TPU v7x, 32 devices: a whole 2x2x4 slice. The times are simulated.
32 devices in a mesh: streams: 2 (over y), span: 4 (over z), head: 2 (over x), seq: 2 (over core).
Axes of the slice: x: 2, y: 2, z: 4, core: 2. Of those that a mesh axis runs over, the one named last changes fastest.
Arguments:
- query_rows: bfloat16 [4096, 1280], P(('streams', 'span', 'seq'), 'head'), parts along dimension 0, may hold values from -100 to 100
- key_rows: bfloat16 [4096, 1280], P(('streams', 'span', 'seq'), 'head'), parts along dimension 0, may hold values from -5 to 5
- value_rows: bfloat16 [4096, 1280], P(('streams', 'span', 'seq'), 'head'), parts along dimension 0, may hold values from -6 to 6
- out_weight: bfloat16 [1280, 5120], P('head', 'seq'), may hold values from -0.59765625 to 0.59765625
- gate_table: float32 [4, 5120], P(None, 'head'), may hold values from 0.5 to 2
- step_index: int32 [8], P('streams'), parts along dimension 0, may hold values from 0 to 3
- block_mask: int32 [8, 4], P('streams'), parts along dimension 0, may hold values from 0 to 1, as said below
Outputs:
- gated_update: bfloat16 [4096, 5120], P(('streams', 'span', 'seq'), 'head'), parts along dimension 0
There are 2 independent parts, one for each index of `streams`. A program takes and returns all parts, laid end to end along the dimension named above; an argument that names none is the same for every part. Nothing has to cross between parts.
Inputs may be any that keep to these rules, and one draw needn't show every extreme that they name: block_mask[c, c] = 1 and block_mask[c, e] = 0 for e > c; entries below the diagonal are 0 or 1.
All inputs are finite; a program needn't handle non-finite values.
Results may differ from a plain program's by a relative error of at most 0.017.
Values may be sent and summed in bfloat16 or wider, within the bound.
No kernel may reach another device: no remote copies, remote signals or barrier semaphores. Data moves between devices by JAX's collectives and lax.ppermute only.
A program may use at most 192 MiB of HBM per device.

v0:
```python
import functools
import math

import jax
import jax.numpy as jnp
from jax import lax
from jax.experimental import pallas as pl
from jax.experimental.pallas import tpu as pltpu
from jax.sharding import PartitionSpec as P

HD = 128
NEG = -1e30
STAT = 16
VMEM_LIMIT = 16 * 1024 * 1024
BRIEF = pl.CostEstimate(flops=1, transcendentals=0, bytes_accessed=1)


def dot(a, b, dims):
    return lax.dot_general(a, b, (dims, ((), ())), preferred_element_type=jnp.float32)


def parts_of(x):
    hi = x.astype(jnp.bfloat16)
    rest = x - hi.astype(jnp.float32)
    mid = rest.astype(jnp.bfloat16)
    low = (rest - mid.astype(jnp.float32)).astype(jnp.bfloat16)
    return hi, mid, low


def write_message(acc, top, out_ref, at):
    rows = acc.shape[0]
    lanes = slice(at, at + HD)
    total = acc[:, HD:]
    live = total > 0.0
    safe = jnp.where(live, total, 1.0)
    out_ref[0:rows, lanes] = (acc[:, :HD] / safe).astype(jnp.bfloat16)
    lse = jnp.where(live, top + jnp.log2(safe), NEG)
    hi, mid, low = parts_of(lse)
    lane = lax.broadcasted_iota(jnp.int32, lse.shape, 1)
    zero = jnp.zeros_like(hi)
    packed = jnp.where(lane == 0, hi, jnp.where(lane == 1, mid, jnp.where(lane == 2, low, zero)))
    row = lax.broadcasted_iota(jnp.int32, (STAT, HD), 0)
    col = lax.broadcasted_iota(jnp.int32, (STAT, HD), 1)
    stats = jnp.zeros((STAT, HD), jnp.float32)
    for block in range(rows // HD):
        pick = jnp.where((row - 3 * block == col) & (col < 3), 1.0, 0.0).astype(jnp.bfloat16)
        stats += dot(pick, packed[block * HD : (block + 1) * HD], ((1,), (1,)))
    out_ref[rows:, lanes] = stats.astype(jnp.bfloat16)


def read_message(msg_ref, rows, at):
    lanes = slice(at, at + HD)
    row = lax.broadcasted_iota(jnp.int32, (STAT, HD), 0)
    blocks = []
    for block in range(rows // HD):
        pick = jnp.where((row >= 3 * block) & (row < 3 * block + 3), 1.0, 0.0).astype(jnp.bfloat16)
        blocks.append(dot(msg_ref[rows:, lanes], pick, ((0,), (0,))))
    return msg_ref[0:rows, lanes].astype(jnp.float32), jnp.concatenate(blocks, axis=0)


def visible_of(role, step, mask_ref):
    span, spans = lax.axis_index("span"), mask_ref.shape[1]
    keys = jnp.maximum(span - step, 0)
    if role == "own":
        there = (span >= step) if step == 0 else (span >= step) & (span != spans - 1)
        return there & (mask_ref[span, keys] == 1)
    return (span == spans - 2) & (span >= step) & (mask_ref[spans - 1, keys] == 1)


def wide(h):
    return slice(2 * h * HD, 2 * (h + 1) * HD)


def update(q, keys, values, acc, top):
    scale = math.log2(math.e) / math.sqrt(HD)
    scores = [dot(q, k, ((1,), (1,))) for k in keys]
    peak = functools.reduce(jnp.maximum, scores) if len(scores) > 1 else scores[0]
    peak = jnp.broadcast_to(jnp.max(peak, axis=1, keepdims=True) * scale, (q.shape[0], HD))
    new_top = peak if top is None else jnp.maximum(top, peak)
    total = None
    for score, v in zip(scores, values):
        line = jnp.concatenate([new_top] * (v.shape[0] // HD), axis=1)
        prob = jnp.exp2(score * scale - line).astype(jnp.bfloat16)
        wide_v = jnp.concatenate([v, jnp.ones(v.shape, jnp.bfloat16)], axis=1)
        term = dot(prob, wide_v, ((1,), (0,)))
        total = term if total is None else total + term
    if top is not None:
        fade = jnp.exp2(top - new_top)
        total += acc * jnp.concatenate([fade, fade], axis=1)
    return total, new_top


def merge(acc, top, part, lse):
    peak = jnp.maximum(top, lse)
    mine = jnp.exp2(top - peak)
    theirs = jnp.where(lse > 0.5 * NEG, jnp.exp2(lse - peak), 0.0)
    return (
        acc * jnp.concatenate([mine, mine], axis=1) + jnp.concatenate([part * theirs, theirs], axis=1),
        peak,
    )


def tall(h):
    return slice(h * HD, (h + 1) * HD)


def attend_kernel(roles, step, emit, mask_ref, k_ref, v_ref, *refs):
    q_refs, refs = refs[: 2 * len(roles)], refs[2 * len(roles) :]
    if step:
        refs = refs[2 * len(roles) :]
    drafts = refs[2 * len(roles) :]
    rows, heads = q_refs[0].shape[0], k_ref.shape[1] // HD
    for i, role in enumerate(roles):
        acc_ref, top_ref = refs[2 * i : 2 * i + 2]
        visible = visible_of(role, step, mask_ref)

        @pl.when(visible)
        def _():
            for h in range(heads):
                for half in range(2):
                    at = slice(half * rows, (half + 1) * rows)
                    acc, top = (acc_ref[at, wide(h)], top_ref[at, tall(h)]) if step else (None, None)
                    acc, top = update(q_refs[2 * i + half][:, tall(h)], [k_ref[:, tall(h)]], [v_ref[:, tall(h)]], acc, top)
                    acc_ref[at, wide(h)] = acc
                    top_ref[at, tall(h)] = top

        if step == 0:

            @pl.when(jnp.logical_not(visible))
            def _():
                acc_ref[...] = jnp.zeros(acc_ref.shape, jnp.float32)
                top_ref[...] = jnp.full(top_ref.shape, NEG, jnp.float32)

        if emit:
            def write():
                for h in range(heads):
                    write_message(acc_ref[rows:, wide(h)], top_ref[rows:, tall(h)], drafts[i], h * HD)

            if role == "lent":
                pl.when(lax.axis_index("span") == mask_ref.shape[1] - 2)(write)
            else:
                write()


def call(kernel, name, out_shape, mask, operands, aliases=None):
    return pl.pallas_call(
        kernel,
        out_shape=out_shape,
        in_specs=[pl.BlockSpec(memory_space=pltpu.SMEM)] + [pl.BlockSpec(memory_space=pltpu.VMEM)] * len(operands),
        out_specs=[pl.BlockSpec(memory_space=pltpu.VMEM)] * len(out_shape),
        input_output_aliases=aliases or {},
        compiler_params=pltpu.CompilerParams(vmem_limit_bytes=VMEM_LIMIT),
        cost_estimate=BRIEF,
        name=name,
    )(mask, *operands)


def state_shape(rows, width):
    return [
        jax.ShapeDtypeStruct((rows, 2 * width), jnp.float32),
        jax.ShapeDtypeStruct((rows, width), jnp.float32),
    ]


def message_shape(rows, heads):
    return jax.ShapeDtypeStruct((rows + STAT, heads * HD), jnp.bfloat16)


def attend(mask, roles, step, key, value, queries, states, emit):
    rows, width = key.shape
    out_shape = state_shape(2 * rows, width) * len(roles)
    if emit:
        out_shape = out_shape + [message_shape(rows, width // HD)] * len(roles)
    operands = [key, value, *queries]
    aliases = {}
    if step:
        aliases = {1 + len(operands) + i: i for i in range(2 * len(roles))}
        for state in states:
            operands += list(state)
    kernel = functools.partial(attend_kernel, roles, step, emit)
    out = call(kernel, "attend_" + "_".join(roles) + str(step), out_shape, mask, operands, aliases)
    return [tuple(out[2 * i : 2 * i + 2]) for i in range(len(roles))], out[2 * len(roles) :]


def fold_kernel(roles, mask_ref, *refs):
    count = len(roles)
    for i, role in enumerate(roles):
        acc_in, top_in, mate_ref = refs[3 * i : 3 * i + 3]
        acc_ref, top_ref = refs[3 * count + 2 * i : 3 * count + 2 * i + 2]
        rows = acc_ref.shape[0]

        def run():
            for h in range(top_ref.shape[1] // HD):
                part, lse = read_message(mate_ref, rows, h * HD)
                acc, top = merge(acc_in[0:rows, wide(h)], top_in[0:rows, tall(h)], part, lse)
                acc_ref[:, wide(h)] = acc
                top_ref[:, tall(h)] = top

        if role == "lent":
            pl.when(lax.axis_index("span") == mask_ref.shape[1] - 2)(run)
        else:
            run()


def fold(mask, roles, states, mates):
    rows, width = mates[0].shape[0] - STAT, mates[0].shape[1]
    operands = [x for state, mate in zip(states, mates) for x in (*state, mate)]
    kernel = functools.partial(fold_kernel, roles)
    out = call(kernel, "fold", state_shape(rows, width) * len(roles), mask, operands)
    return [tuple(out[2 * i : 2 * i + 2]) for i in range(len(roles))]


def last_kernel(role, step, groups, mask_ref, ka_ref, kb_ref, va_ref, vb_ref, q_ref, acc_in, top_in, *outs):
    rows = q_ref.shape[0]
    visible = visible_of(role, step, mask_ref)

    def store(h, acc, top):
        if role == "own":
            outs[0][:, wide(h)] = acc
            outs[1][:, tall(h)] = top
        else:
            g = 0 if h < groups[1][0] else 1
            write_message(acc, top, outs[g], (h - groups[g][0]) * HD)

    def run(see):
        for h in range(q_ref.shape[1] // HD):
            acc, top = acc_in[:, wide(h)], top_in[:, tall(h)]
            if see:
                keys, values = [ka_ref[:, tall(h)], kb_ref[:, tall(h)]], [va_ref[:, tall(h)], vb_ref[:, tall(h)]]
                acc, top = update(q_ref[:, tall(h)], keys, values, acc, top)
            store(h, acc, top)

    helps = lax.axis_index("span") == mask_ref.shape[1] - 2
    pl.when(visible)(lambda: run(True))
    pl.when(jnp.logical_not(visible) & (helps if role == "lent" else True))(lambda: run(False))


def attend_last(mask, role, step, groups, keys, values, query, state):
    rows, width = query.shape
    if role == "own":
        out_shape = state_shape(rows, width)
    else:
        out_shape = [message_shape(rows, b - a) for a, b in groups]
    kernel = functools.partial(last_kernel, role, step, groups)
    return call(kernel, "last_" + role, out_shape, mask, [*keys, *values, query, *state])


def join_kernel(part_of_heads, mask_ref, acc_ref, top_ref, msg_ref, out_ref):
    low, high = part_of_heads
    rows = acc_ref.shape[0]

    def run(helped):
        for h in range(low, high):
            acc = acc_ref[:, wide(h)]
            if helped:
                part, lse = read_message(msg_ref, rows, (h - low) * HD)
                acc, _ = merge(acc, top_ref[:, tall(h)], part, lse)
            out_ref[:, tall(h - low)] = (acc[:, :HD] / acc[:, HD:]).astype(jnp.bfloat16)

    helped = lax.axis_index("span") == mask_ref.shape[1] - 1
    pl.when(helped)(lambda: run(True))
    pl.when(jnp.logical_not(helped))(lambda: run(False))


def join(mask, part_of_heads, state, message):
    shape = (state[0].shape[0], (part_of_heads[1] - part_of_heads[0]) * HD)
    kernel = functools.partial(join_kernel, part_of_heads)
    return call(kernel, "join" + str(part_of_heads[0]), [jax.ShapeDtypeStruct(shape, jnp.bfloat16)], mask, [*state, message])[0]


TILE = 512


def project_kernel(lows, step_ref, *refs):
    count = len(lows)
    rows_refs, (w_own, w_mate, w_far, w_back), refs = refs[:count], refs[count : count + 4], refs[count + 4 :]
    straight = lax.axis_index("head") == lax.axis_index("seq")
    last = len(refs) > 1
    if last:
        total_ref, gate_ref, out_ref, stage, sems = refs
        gate_row = pl.ds(step_ref[lax.axis_index("span")], 1)
    else:
        out_ref = refs[0]
    tiles = out_ref.shape[1] // TILE

    def copy(t):
        return pltpu.make_async_copy(stage.at[t], out_ref.at[:, t * TILE : (t + 1) * TILE], sems.at[t])

    def run(w_mine, w_theirs):
        for t in range(tiles):
            lanes = slice(t * TILE, (t + 1) * TILE)
            total = total_ref[:, lanes] if last else None
            for ref, (low, own) in zip(rows_refs, lows):
                weight = w_mine if own else w_theirs
                term = dot(ref[...], weight[low : low + ref.shape[1], lanes], ((1,), (0,)))
                total = term if total is None else total + term
            if last:
                stage[t] = (gate_ref[gate_row, lanes] * total).astype(jnp.bfloat16)
                copy(t).start()
            else:
                out_ref[:, lanes] = total

    pl.when(straight)(lambda: run(w_own, w_back))
    pl.when(jnp.logical_not(straight))(lambda: run(w_mate, w_far))
    if last:
        for t in range(tiles):
            copy(t).wait()


def project(step_index, terms, weights, total=None, gate_table=None):
    rows, columns = terms[0][0].shape[0], weights[0].shape[1]
    last = total is not None
    operands = [x for x, _, _ in terms] + [*weights] + ([total, gate_table] if last else [])
    return pl.pallas_call(
        functools.partial(project_kernel, [(low, own) for _, low, own in terms]),
        out_shape=jax.ShapeDtypeStruct((rows, columns), jnp.bfloat16 if last else jnp.float32),
        in_specs=[pl.BlockSpec(memory_space=pltpu.SMEM)]
        + [pl.BlockSpec(memory_space=pltpu.VMEM)] * len(operands),
        out_specs=pl.BlockSpec(memory_space=pl.ANY if last else pltpu.VMEM),
        scratch_shapes=[
            pltpu.VMEM((columns // TILE, rows, TILE), jnp.bfloat16),
            pltpu.SemaphoreType.DMA((columns // TILE,)),
        ]
        if last
        else [],
        compiler_params=pltpu.CompilerParams(vmem_limit_bytes=VMEM_LIMIT),
        cost_estimate=BRIEF,
        name="project_last" if last else "project_most",
    )(step_index, *operands)


def after(value, done):
    return lax.optimization_barrier((value, done))[0]


def swap_pairs(count):
    return [(i, count - 1 - i) for i in range(count)]


def on_device(query_rows, key_rows, value_rows, out_weight, gate_table, step_index, block_mask):
    heads = query_rows.shape[1] // HD
    spans, cores, sides = lax.axis_size("span"), lax.axis_size("seq"), lax.axis_size("head")
    split = (heads + 1) // 2
    groups = [(0, split), (split, heads)]
    exchange = sides == cores == 2
    final = spans - 2

    def up(x, step):
        return lax.ppermute(x, "span", [(i, i + 1) for i in range(step - 1, spans - 2)])

    def across(x):
        return lax.ppermute(x, "seq", swap_pairs(cores))

    if exchange:
        pair = ("head", "seq")
        w_far = lax.ppermute(out_weight, pair, [(1, 2), (2, 1)])
    asked = lax.ppermute(query_rows, "span", [(spans - 1, spans - 2)])
    query_mate = across(query_rows)
    if exchange:
        w_mate = across(out_weight)
        query_mate = after(query_mate, w_mate)
    queries, lent = [query_rows, query_mate], None
    key, value = key_rows, value_rows
    roles = ["lent", "own"]
    for step in range(final):
        key_next, value_next = up(key, step + 1), up(value, step + 1)
        emit = step + 1 == final
        if step == 0:
            (own,), own_draft = attend(block_mask, ["own"], 0, key, value, queries, [], emit)
            asked = after(asked, own)
            asks = [asked, across(asked)]
            (lent,), lent_draft = attend(block_mask, ["lent"], 0, key, value, asks, [], emit)
            states, drafts = [lent, own], [*lent_draft, *own_draft]
        else:
            states, drafts = attend(block_mask, roles, step, key, value, asks + queries, states, emit)
        key, value = key_next, value_next
    lent, own = fold(block_mask, roles, states, [across(x) for x in drafts])
    keys = [key, across(key)]
    values = [value, across(value)]
    back_up = [(spans - 2, spans - 1)]
    messages = attend_last(block_mask, "lent", final, groups, keys, values, asks[0], lent)
    sent = [lax.ppermute(x, "span", back_up) for x in messages]
    if exchange:
        w_back = across(after(w_far, messages[1]))
    own = attend_last(block_mask, "own", final, groups, keys, values, after(query_rows, messages), own)
    mine = [join(block_mask, groups[0], own, sent[0])]
    mine.append(join(block_mask, groups[1], own, after(sent[1], mine[0])))

    if exchange:
        theirs = [lax.ppermute(x, "head", swap_pairs(sides)) for x in mine]
        weights, low = [out_weight, w_mate, w_far, w_back], split * HD
        most = [(mine[0], 0, True), (mine[1], low, True), (theirs[0], 0, False)]
        total = project(step_index, most, weights)
        return project(step_index, [(theirs[1], low, False)], weights, total, gate_table)
    weight = lax.all_gather(out_weight, "seq", axis=1, tiled=True)
    projected = jnp.dot(jnp.concatenate(mine, axis=1), weight, preferred_element_type=jnp.float32)
    shared = lax.psum_scatter(projected.astype(jnp.bfloat16), "head", scatter_dimension=1, tiled=True)
    gate_row = gate_table[step_index[lax.axis_index("span")]]
    return (gate_row[None, :] * shared.astype(jnp.float32)).astype(jnp.bfloat16)


def solution(mesh):
    in_specs = (
        P(("streams", "span", "seq"), "head"),
        P(("streams", "span", "seq"), "head"),
        P(("streams", "span", "seq"), "head"),
        P("head", "seq"),
        P(None, "head"),
        P("streams"),
        P("streams", None),
    )
    out_specs = P(("streams", "span", "seq"), "head")
    return jax.shard_map(
        on_device, mesh=mesh, in_specs=in_specs, out_specs=out_specs, check_vma=False
    )
```

profile of v0, /device:TPU:28, one launch (start us, length us, event | category | flops | bytes accessed | tf_op | source)
XLA Modules:
  0.0 63.3 jit_solution(2692188683728958105)
XLA Ops:
  0.0 0.9 %collective-permute-start.15 = (bf16[640,2560]{1,0:T(8,128)(2,1)}, bf16[640,2560]{1,0:T(8,128)(2,1)S(1)}, u32[]{:S(2)}, u32[]{:S(2)}) collective-permute-start(bf16[640,2560]{1,0:T(8,128)(2,1)} %refs_1_.1), channel_id=1, source_target_pairs={{1,2},{2,1},{5,6},{6,5},{9,10},{10,9},{13,14},{14,13},{17,18},{18,... | collective-permute-start | bytes 9830408 | tf_op jit(solution)/shard_map/ppermute | solution.py:356
  0.9 2.7 %collective-permute-start.7 = (bf16[256,640]{1,0:T(8,128)(2,1)}, bf16[256,640]{1,0:T(8,128)(2,1)S(1)}, u32[]{:S(2)}, u32[]{:S(2)}) collective-permute-start(bf16[256,640]{1,0:T(8,128)(2,1)} %q_ref), channel_id=1, source_target_pairs={{0,1},{1,0},{2,3},{3,2},{4,5},{5,4},{6,7},{7,6},{8,9},{9,8},{10,11... | collective-permute-start | bytes 983048 | tf_op jit(solution)/shard_map/ppermute | solution.py:352
  3.6 2.4 %collective-permute-start.6 = (bf16[256,640]{1,0:T(8,128)(2,1)}, bf16[256,640]{1,0:T(8,128)(2,1)S(1)}, u32[]{:S(2)}, u32[]{:S(2)}) collective-permute-start(bf16[256,640]{1,0:T(8,128)(2,1)} %q_ref), channel_id=1, source_target_pairs={{12,8},{13,9},{14,10},{15,11},{28,24},{29,25},{30,26},{31,27}} | collective-permute-start | bytes 983048 | tf_op jit(solution)/shard_map/ppermute | solution.py:357
  6.0 0.7 %collective-permute-start = (bf16[256,640]{1,0:T(8,128)(2,1)}, bf16[256,640]{1,0:T(8,128)(2,1)S(1)}, u32[]{:S(2)}, u32[]{:S(2)}) collective-permute-start(bf16[256,640]{1,0:T(8,128)(2,1)} %k_ref.3), channel_id=1, source_target_pairs={{0,4},{4,8},{1,5},{5,9},{2,6},{6,10},{3,7},{7,11},{16,20},{20,24},... | collective-permute-start | bytes 983048 | tf_op jit(solution)/shard_map/ppermute | solution.py:349
  6.7 0.7 %collective-permute-start.3 = (bf16[256,640]{1,0:T(8,128)(2,1)}, bf16[256,640]{1,0:T(8,128)(2,1)S(1)}, u32[]{:S(2)}, u32[]{:S(2)}) collective-permute-start(bf16[256,640]{1,0:T(8,128)(2,1)} %v_ref.3), channel_id=1, source_target_pairs={{0,4},{4,8},{1,5},{5,9},{2,6},{6,10},{3,7},{7,11},{16,20},{20,24},... | collective-permute-start | bytes 983048 | tf_op jit(solution)/shard_map/ppermute | solution.py:349
  7.4 1.0 %copy-done.1 = bf16[256,640]{1,0:T(8,128)(2,1)S(1)} copy-done((bf16[256,640]{1,0:T(8,128)(2,1)S(1)}, bf16[256,640]{1,0:T(8,128)(2,1)}, u32[]{:S(2)}) %copy-start.1) | copy-done | bytes 327704
  8.3 1.0 %copy-done.3 = bf16[256,640]{1,0:T(8,128)(2,1)S(1)} copy-done((bf16[256,640]{1,0:T(8,128)(2,1)S(1)}, bf16[256,640]{1,0:T(8,128)(2,1)}, u32[]{:S(2)}) %copy-start.3) | copy-done | bytes 327704
  9.3 1.0 %copy-done.4 = bf16[256,640]{1,0:T(8,128)(2,1)S(1)} copy-done((bf16[256,640]{1,0:T(8,128)(2,1)S(1)}, bf16[256,640]{1,0:T(8,128)(2,1)}, u32[]{:S(2)}) %copy-start.4) | copy-done | bytes 327704
  10.3 0.7 %copy-done.5 = s32[4,4]{1,0:T(4,128)S(1)} copy-done((s32[4,4]{1,0:T(4,128)S(1)}, s32[4,4]{1,0:T(4,128)}, u32[]{:S(2)}) %copy-start.5) | copy-done | bytes 88
  11.0 1.6 %attend_own0.1 = (f32[512,1280]{1,0:T(8,128)S(1)}, f32[512,640]{1,0:T(8,128)S(1)}) custom-call(s32[4,4]{1,0:T(4,128)S(1)} %copy-done.5, bf16[256,640]{1,0:T(8,128)(2,1)S(1)} %copy-done.3, bf16[256,640]{1,0:T(8,128)(2,1)S(1)} %copy-done.4, bf16[256,640]{1,0:T(8,128)(2,1)S(1)} %copy-done.1, bf16[256,640]{1,0:T(8,128)(2,1)S(1)} %collective-permute-done.7.refs_1_.refs_3_), custom_call_target="tpu_custom_call" | custom-call | flops 1 | bytes 1 | tf_op jit(solution)/shard_map/attend_own0/pallas_call | solution.py:146
  12.6 0.8 %collective-permute-done.6.refs_0_.q_ref = bf16[256,640]{1,0:T(8,128)(2,1)S(1)} collective-permute-done((bf16[256,640]{1,0:T(8,128)(2,1)}, bf16[256,640]{1,0:T(8,128)(2,1)S(1)}, u32[]{:S(2)}, u32[]{:S(2)}) %collective-permute-start.6) | collective-permute-done | bytes 327712 | tf_op jit(solution)/shard_map/ppermute | solution.py:357
  13.4 0.7 %collective-permute-start.1 = (bf16[256,640]{1,0:T(8,128)(2,1)S(1)}, bf16[256,640]{1,0:T(8,128)(2,1)S(1)}, u32[]{:S(2)}, u32[]{:S(2)}) collective-permute-start(bf16[256,640]{1,0:T(8,128)(2,1)S(1)} %collective-permute-done.k_ref), channel_id=1, source_target_pairs={{4,8},{5,9},{6,10},{7,11},{20,24},{21,25},{22,26},{23,27}} | collective-permute-start | bytes 983048 | tf_op jit(solution)/shard_map/ppermute | solution.py:349
  14.1 0.7 %collective-permute-start.4 = (bf16[256,640]{1,0:T(8,128)(2,1)S(1)}, bf16[256,640]{1,0:T(8,128)(2,1)S(1)}, u32[]{:S(2)}, u32[]{:S(2)}) collective-permute-start(bf16[256,640]{1,0:T(8,128)(2,1)S(1)} %collective-permute-done.3.v_ref), channel_id=1, source_target_pairs={{4,8},{5,9},{6,10},{7,11},{20,24},{21,25},{22,26},{23,27}} | collective-permute-start | bytes 983048 | tf_op jit(solution)/shard_map/ppermute | solution.py:349
  15.0 0.8 %attend_lent0.1 = (f32[512,1280]{1,0:T(8,128)S(1)}, f32[512,640]{1,0:T(8,128)S(1)}) custom-call(s32[4,4]{1,0:T(4,128)S(1)} %copy-done.5, bf16[256,640]{1,0:T(8,128)(2,1)S(1)} %copy-done.3, bf16[256,640]{1,0:T(8,128)(2,1)S(1)} %copy-done.4, bf16[256,640]{1,0:T(8,128)(2,1)S(1)} %collective-permute-done.6.refs_0_.q_ref, ...), custom_call_target="tpu_custom_call" | custom-call | flops 1 | bytes 1 | tf_op jit(solution)/shard_map/attend_lent0/pallas_call | solution.py:146
  15.9 1.1 %attend_lent_own1.1 = (f32[512,1280]{1,0:T(8,128)S(1)}, f32[512,640]{1,0:T(8,128)S(1)}, f32[512,1280]{1,0:T(8,128)S(1)}, f32[512,640]{1,0:T(8,128)S(1)}, bf16[27...) custom-call(s32[4,4]{1,0:T(4,128)S(1)} %copy-done.5, ...), custom_call_target="tpu_custom_call", output_to_operand_aliasing={{0}: (7, {}), {1}: (8, {}), {2}: (9, {}), {3}: (10, {})} | custom-call | flops 1 | bytes 1 | tf_op jit(solution)/shard_map/attend_lent_own1/pallas_call | solution.py:146
  18.0 0.6 collective-permute-done.10.refs_2_
  18.6 0.5 collective-permute-done.11.refs_5_
  19.1 1.1 %fold.1 = (f32[256,1280]{1,0:T(8,128)S(1)}, f32[256,640]{1,0:T(8,128)S(1)}, f32[256,1280]{1,0:T(8,128)S(1)}, f32[256,640]{1,0:T(8,128)S(1)}) custom-call(s32[4,4]{1,0:T(4,128)S(1)} %copy-done.5, f32[512,1280]{1,0:T(8,128)S(1)} %get-tuple-element.34.refs_0_, f32[512,640]{1,0:T(8,128)S(1)} %get-tuple-element.35.refs_1_, ...), custom_call_target="tpu_custom_call" | custom-call | flops 1 | bytes 1 | tf_op jit(solution)/shard_map/fold/pallas_call | solution.py:146
  20.2 0.6 last_lent.1
  20.8 19.9 %collective-permute-start.16 = (bf16[640,2560]{1,0:T(8,128)(2,1)S(1)}, bf16[640,2560]{1,0:T(8,128)(2,1)S(1)}, u32[]{:S(2)}, u32[]{:S(2)}) collective-permute-start(bf16[640,2560]{1,0:T(8,128)(2,1)S(1)} %collective-permute-done.15.refs_5_.refs_3_), channel_id=1, source_target_pairs={{0,1},{1,0},{2,3},{3,2},{4,5},{5,4},{6,7},{7,6},{8,9},{9,8},{10,11... | collective-permute-start | bytes 9830408 | tf_op jit(solution)/shard_map/ppermute | solution.py:352
  40.7 1.3 %collective-permute-start.13 = (bf16[272,384]{1,0:T(8,128)(2,1)S(1)}, bf16[272,384]{1,0:T(8,128)(2,1)S(1)}, u32[]{:S(2)}, u32[]{:S(2)}) collective-permute-start(bf16[272,384]{1,0:T(8,128)(2,1)S(1)} %get-tuple-element.42), channel_id=1, source_target_pairs={{8,12},{9,13},{10,14},{11,15},{24,28},{25,29},{26,30},{27,31}} | collective-permute-start | bytes 626696 | tf_op jit(solution)/shard_map/ppermute | solution.py:382
  42.0 1.3 %collective-permute-start.12 = (bf16[272,256]{1,0:T(8,128)(2,1)S(1)}, bf16[272,256]{1,0:T(8,128)(2,1)S(1)}, u32[]{:S(2)}, u32[]{:S(2)}) collective-permute-start(bf16[272,256]{1,0:T(8,128)(2,1)S(1)} %get-tuple-element.43), channel_id=1, source_target_pairs={{8,12},{9,13},{10,14},{11,15},{24,28},{25,29},{26,30},{27,31}} | collective-permute-start | bytes 417800 | tf_op jit(solution)/shard_map/ppermute | solution.py:382
  43.3 0.7 %last_own.1 = (f32[256,1280]{1,0:T(8,128)S(1)}, f32[256,640]{1,0:T(8,128)S(1)}) custom-call(s32[4,4]{1,0:T(4,128)S(1)} %copy-done.5, bf16[256,640]{1,0:T(8,128)(2,1)S(1)} %collective-permute-done.1.ka_ref, bf16[256,640]{1,0:T(8,128)(2,1)S(1)} %collective-permute-done.2.kb_ref, bf16[256,640]{1,0:T(8,128)(2,1)S(1)} %collective-permute-done.4.va_ref, ...), custom_call_target="tpu_custom_call" | custom-call | flops 1 | bytes 1 | tf_op jit(solution)/shard_map/last_own/pallas_call | solution.py:146
  44.0 6.9 %collective-permute-done.13.msg_ref = bf16[272,384]{1,0:T(8,128)(2,1)S(1)} collective-permute-done((bf16[272,384]{1,0:T(8,128)(2,1)S(1)}, bf16[272,384]{1,0:T(8,128)(2,1)S(1)}, u32[]{:S(2)}, u32[]{:S(2)}) %collective-permute-start.13) | collective-permute-done | bytes 208928 | tf_op jit(solution)/shard_map/ppermute | solution.py:382
  50.9 1.0 %join0.1.refs_0_ = bf16[256,384]{1,0:T(8,128)(2,1)S(1)} custom-call(s32[4,4]{1,0:T(4,128)S(1)} %copy-done.5, f32[256,1280]{1,0:T(8,128)S(1)} %get-tuple-element.47.acc_ref, f32[256,640]{1,0:T(8,128)S(1)} %get-tuple-element.48.top_ref, bf16[272,384]{1,0:T(8,128)(2,1)S(1)} %collective-permute-done.13.msg_ref), custom_call_target="tpu_custom_call" | custom-call | flops 1 | bytes 1 | tf_op jit(solution)/shard_map/join0/pallas_call | solution.py:146
  51.9 1.1 %collective-permute-start.17 = (bf16[256,384]{1,0:T(8,128)(2,1)S(1)}, bf16[256,384]{1,0:T(8,128)(2,1)S(1)}, u32[]{:S(2)}, u32[]{:S(2)}) collective-permute-start(bf16[256,384]{1,0:T(8,128)(2,1)S(1)} %join0.1.refs_0_), channel_id=1, source_target_pairs={{0,2},{2,0},{1,3},{3,1},{4,6},{6,4},{5,7},{7,5},{8,10},{10,8},{9,1... | collective-permute-start | bytes 589832 | tf_op jit(solution)/shard_map/ppermute | solution.py:390
  53.0 0.4 collective-permute-done.12.msg_ref
  53.3 1.1 %join3.1.refs_1_ = bf16[256,256]{1,0:T(8,128)(2,1)S(1)} custom-call(s32[4,4]{1,0:T(4,128)S(1)} %copy-done.5, f32[256,1280]{1,0:T(8,128)S(1)} %get-tuple-element.47.acc_ref, f32[256,640]{1,0:T(8,128)S(1)} %get-tuple-element.48.top_ref, bf16[272,256]{1,0:T(8,128)(2,1)S(1)} %collective-permute-done.12.msg_ref), custom_call_target="tpu_custom_call" | custom-call | flops 1 | bytes 1 | tf_op jit(solution)/shard_map/join3/pallas_call | solution.py:146
  54.4 1.1 %collective-permute-start.14 = (bf16[256,256]{1,0:T(8,128)(2,1)S(1)}, bf16[256,256]{1,0:T(8,128)(2,1)S(1)}, u32[]{:S(2)}, u32[]{:S(2)}) collective-permute-start(bf16[256,256]{1,0:T(8,128)(2,1)S(1)} %join3.1.refs_1_), channel_id=1, source_target_pairs={{0,2},{2,0},{1,3},{3,1},{4,6},{6,4},{5,7},{7,5},{8,10},{10,8},{9,1... | collective-permute-start | bytes 393224 | tf_op jit(solution)/shard_map/ppermute | solution.py:390
  55.5 3.3 %collective-permute-done.17.refs_2_ = bf16[256,384]{1,0:T(8,128)(2,1)S(1)} collective-permute-done((bf16[256,384]{1,0:T(8,128)(2,1)S(1)}, bf16[256,384]{1,0:T(8,128)(2,1)S(1)}, u32[]{:S(2)}, u32[]{:S(2)}) %collective-permute-start.17) | collective-permute-done | bytes 196640 | tf_op jit(solution)/shard_map/ppermute | solution.py:390
  58.8 2.4 %project_most.1.refs_5_ = f32[256,2560]{1,0:T(8,128)S(1)} custom-call(s32[4]{0:T(128)S(1)} %copy-done.7, bf16[256,384]{1,0:T(8,128)(2,1)S(1)} %join0.1.refs_0_, bf16[256,256]{1,0:T(8,128)(2,1)S(1)} %join3.1.refs_1_, bf16[256,384]{1,0:T(8,128)(2,1)S(1)} %collective-permute-done.17.refs_2_, bf16[640,2560]{1,0:T(8,128)(2,1)S(1)} %copy-done, ...), custom_call_target="tpu_custom_call" | custom-call | flops 1 | bytes 1 | tf_op jit(solution)/shard_map/project_most/pallas_call | solution.py:314
  61.3 1.9 %project_last.1 = bf16[256,2560]{1,0:T(8,128)(2,1)} custom-call(s32[4]{0:T(128)S(1)} %copy-done.7, bf16[256,256]{1,0:T(8,128)(2,1)S(1)} %collective-permute-done.14.refs_0_, bf16[640,2560]{1,0:T(8,128)(2,1)S(1)} %copy-done, bf16[640,2560]{1,0:T(8,128)(2,1)S(1)} %collective-permute-done.8.refs_4_.refs_2_, ...), custom_call_target="tpu_custom_call" | custom-call | flops 1 | bytes 1 | tf_op jit(solution)/shard_map/project_last/pallas_call | solution.py:314
  (30 shorter events, 1.3 us)
Async XLA Ops:
  0.0 7.3 %collective-permute-start.8 = (bf16[640,2560]{1,0:T(8,128)(2,1)}, bf16[640,2560]{1,0:T(8,128)(2,1)S(1)}, u32[]{:S(2)}, u32[]{:S(2)}) collective-permute-start(bf16[640,2560]{1,0:T(8,128)(2,1)} %refs_1_.1), channel_id=1, source_target_pairs={{0,1},{1,0},{2,3},{3,2},{4,5},{5,4},{6,7},{7,6},{8,9},{9,8},{10,11... | collective-permute-start | bytes 9830408 | tf_op jit(solution)/shard_map/ppermute | solution.py:352
  0.0 20.8 %collective-permute-start.15 = (bf16[640,2560]{1,0:T(8,128)(2,1)}, bf16[640,2560]{1,0:T(8,128)(2,1)S(1)}, u32[]{:S(2)}, u32[]{:S(2)}) collective-permute-start(bf16[640,2560]{1,0:T(8,128)(2,1)} %refs_1_.1), channel_id=1, source_target_pairs={{1,2},{2,1},{5,6},{6,5},{9,10},{10,9},{13,14},{14,13},{17,18},{18,... | collective-permute-start | bytes 9830408 | tf_op jit(solution)/shard_map/ppermute | solution.py:356
  0.9 5.8 %collective-permute-start.7 = (bf16[256,640]{1,0:T(8,128)(2,1)}, bf16[256,640]{1,0:T(8,128)(2,1)S(1)}, u32[]{:S(2)}, u32[]{:S(2)}) collective-permute-start(bf16[256,640]{1,0:T(8,128)(2,1)} %q_ref), channel_id=1, source_target_pairs={{0,1},{1,0},{2,3},{3,2},{4,5},{5,4},{6,7},{7,6},{8,9},{9,8},{10,11... | collective-permute-start | bytes 983048 | tf_op jit(solution)/shard_map/ppermute | solution.py:352
  3.6 9.8 %collective-permute-start.6 = (bf16[256,640]{1,0:T(8,128)(2,1)}, bf16[256,640]{1,0:T(8,128)(2,1)S(1)}, u32[]{:S(2)}, u32[]{:S(2)}) collective-permute-start(bf16[256,640]{1,0:T(8,128)(2,1)} %q_ref), channel_id=1, source_target_pairs={{12,8},{13,9},{14,10},{15,11},{28,24},{29,25},{30,26},{31,27}} | collective-permute-start | bytes 983048 | tf_op jit(solution)/shard_map/ppermute | solution.py:357
  6.0 7.4 %collective-permute-start = (bf16[256,640]{1,0:T(8,128)(2,1)}, bf16[256,640]{1,0:T(8,128)(2,1)S(1)}, u32[]{:S(2)}, u32[]{:S(2)}) collective-permute-start(bf16[256,640]{1,0:T(8,128)(2,1)} %k_ref.3), channel_id=1, source_target_pairs={{0,4},{4,8},{1,5},{5,9},{2,6},{6,10},{3,7},{7,11},{16,20},{20,24},... | collective-permute-start | bytes 983048 | tf_op jit(solution)/shard_map/ppermute | solution.py:349
  6.7 7.4 %collective-permute-start.3 = (bf16[256,640]{1,0:T(8,128)(2,1)}, bf16[256,640]{1,0:T(8,128)(2,1)S(1)}, u32[]{:S(2)}, u32[]{:S(2)}) collective-permute-start(bf16[256,640]{1,0:T(8,128)(2,1)} %v_ref.3), channel_id=1, source_target_pairs={{0,4},{4,8},{1,5},{5,9},{2,6},{6,10},{3,7},{7,11},{16,20},{20,24},... | collective-permute-start | bytes 983048 | tf_op jit(solution)/shard_map/ppermute | solution.py:349
  7.4 1.0 %copy-start.1 = (bf16[256,640]{1,0:T(8,128)(2,1)S(1)}, bf16[256,640]{1,0:T(8,128)(2,1)}, u32[]{:S(2)}) copy-start(bf16[256,640]{1,0:T(8,128)(2,1)} %q_ref) | copy-start | bytes 983044
  8.3 1.0 %copy-start.3 = (bf16[256,640]{1,0:T(8,128)(2,1)S(1)}, bf16[256,640]{1,0:T(8,128)(2,1)}, u32[]{:S(2)}) copy-start(bf16[256,640]{1,0:T(8,128)(2,1)} %k_ref.3) | copy-start | bytes 983044
  9.3 1.0 %copy-start.4 = (bf16[256,640]{1,0:T(8,128)(2,1)S(1)}, bf16[256,640]{1,0:T(8,128)(2,1)}, u32[]{:S(2)}) copy-start(bf16[256,640]{1,0:T(8,128)(2,1)} %v_ref.3) | copy-start | bytes 983044
  10.3 0.7 %copy-start.5 = (s32[4,4]{1,0:T(4,128)S(1)}, s32[4,4]{1,0:T(4,128)}, u32[]{:S(2)}) copy-start(s32[4,4]{1,0:T(4,128)} %mask_ref.15) | copy-start | bytes 196
  11.0 4.9 %copy-start.2 = (bf16[256,640]{1,0:T(8,128)(2,1)S(1)}, bf16[256,640]{1,0:T(8,128)(2,1)}, u32[]{:S(2)}) copy-start(bf16[256,640]{1,0:T(8,128)(2,1)} %q_ref) | copy-start | bytes 983044
  13.4 1.6 %collective-permute-start.9 = (bf16[256,640]{1,0:T(8,128)(2,1)S(1)}, bf16[256,640]{1,0:T(8,128)(2,1)S(1)}, u32[]{:S(2)}, u32[]{:S(2)}) collective-permute-start(bf16[256,640]{1,0:T(8,128)(2,1)S(1)} %collective-permute-done.6.refs_0_.q_ref), channel_id=1, source_target_pairs={{0,1},{1,0},{2,3},{3,2},{4,5},{5,4},{6,7},{7,6},{8,9},{9,8},{10,11... | collective-permute-start | bytes 983048 | tf_op jit(solution)/shard_map/ppermute | solution.py:352
  13.4 4.1 %collective-permute-start.1 = (bf16[256,640]{1,0:T(8,128)(2,1)S(1)}, bf16[256,640]{1,0:T(8,128)(2,1)S(1)}, u32[]{:S(2)}, u32[]{:S(2)}) collective-permute-start(bf16[256,640]{1,0:T(8,128)(2,1)S(1)} %collective-permute-done.k_ref), channel_id=1, source_target_pairs={{4,8},{5,9},{6,10},{7,11},{20,24},{21,25},{22,26},{23,27}} | collective-permute-start | bytes 983048 | tf_op jit(solution)/shard_map/ppermute | solution.py:349
  14.1 3.7 %collective-permute-start.4 = (bf16[256,640]{1,0:T(8,128)(2,1)S(1)}, bf16[256,640]{1,0:T(8,128)(2,1)S(1)}, u32[]{:S(2)}, u32[]{:S(2)}) collective-permute-start(bf16[256,640]{1,0:T(8,128)(2,1)S(1)} %collective-permute-done.3.v_ref), channel_id=1, source_target_pairs={{4,8},{5,9},{6,10},{7,11},{20,24},{21,25},{22,26},{23,27}} | collective-permute-start | bytes 983048 | tf_op jit(solution)/shard_map/ppermute | solution.py:349
  16.9 1.7 %collective-permute-start.10 = (bf16[272,640]{1,0:T(8,128)(2,1)S(1)}, bf16[272,640]{1,0:T(8,128)(2,1)S(1)}, u32[]{:S(2)}, u32[]{:S(2)}) collective-permute-start(bf16[272,640]{1,0:T(8,128)(2,1)S(1)} %get-tuple-element.36), channel_id=1, source_target_pairs={{0,1},{1,0},{2,3},{3,2},{4,5},{5,4},{6,7},{7,6},{8,9},{9,8},{10,11... | collective-permute-start | bytes 1044488 | tf_op jit(solution)/shard_map/ppermute | solution.py:352
  17.2 1.9 %collective-permute-start.11 = (bf16[272,640]{1,0:T(8,128)(2,1)S(1)}, bf16[272,640]{1,0:T(8,128)(2,1)S(1)}, u32[]{:S(2)}, u32[]{:S(2)}) collective-permute-start(bf16[272,640]{1,0:T(8,128)(2,1)S(1)} %get-tuple-element.39), channel_id=1, source_target_pairs={{0,1},{1,0},{2,3},{3,2},{4,5},{5,4},{6,7},{7,6},{8,9},{9,8},{10,11... | collective-permute-start | bytes 1044488 | tf_op jit(solution)/shard_map/ppermute | solution.py:352
  17.5 2.7 %collective-permute-start.2 = (bf16[256,640]{1,0:T(8,128)(2,1)S(1)}, bf16[256,640]{1,0:T(8,128)(2,1)S(1)}, u32[]{:S(2)}, u32[]{:S(2)}) collective-permute-start(bf16[256,640]{1,0:T(8,128)(2,1)S(1)} %collective-permute-done.1.ka_ref), channel_id=1, source_target_pairs={{0,1},{1,0},{2,3},{3,2},{4,5},{5,4},{6,7},{7,6},{8,9},{9,8},{10,11... | collective-permute-start | bytes 983048 | tf_op jit(solution)/shard_map/ppermute | solution.py:352
  17.7 2.4 %collective-permute-start.5 = (bf16[256,640]{1,0:T(8,128)(2,1)S(1)}, bf16[256,640]{1,0:T(8,128)(2,1)S(1)}, u32[]{:S(2)}, u32[]{:S(2)}) collective-permute-start(bf16[256,640]{1,0:T(8,128)(2,1)S(1)} %collective-permute-done.4.va_ref), channel_id=1, source_target_pairs={{0,1},{1,0},{2,3},{3,2},{4,5},{5,4},{6,7},{7,6},{8,9},{9,8},{10,11... | collective-permute-start | bytes 983048 | tf_op jit(solution)/shard_map/ppermute | solution.py:352
  20.8 38.0 %collective-permute-start.16 = (bf16[640,2560]{1,0:T(8,128)(2,1)S(1)}, bf16[640,2560]{1,0:T(8,128)(2,1)S(1)}, u32[]{:S(2)}, u32[]{:S(2)}) collective-permute-start(bf16[640,2560]{1,0:T(8,128)(2,1)S(1)} %collective-permute-done.15.refs_5_.refs_3_), channel_id=1, source_target_pairs={{0,1},{1,0},{2,3},{3,2},{4,5},{5,4},{6,7},{7,6},{8,9},{9,8},{10,11... | collective-permute-start | bytes 9830408 | tf_op jit(solution)/shard_map/ppermute | solution.py:352
  40.7 10.2 %collective-permute-start.13 = (bf16[272,384]{1,0:T(8,128)(2,1)S(1)}, bf16[272,384]{1,0:T(8,128)(2,1)S(1)}, u32[]{:S(2)}, u32[]{:S(2)}) collective-permute-start(bf16[272,384]{1,0:T(8,128)(2,1)S(1)} %get-tuple-element.42), channel_id=1, source_target_pairs={{8,12},{9,13},{10,14},{11,15},{24,28},{25,29},{26,30},{27,31}} | collective-permute-start | bytes 626696 | tf_op jit(solution)/shard_map/ppermute | solution.py:382
  42.0 11.3 %collective-permute-start.12 = (bf16[272,256]{1,0:T(8,128)(2,1)S(1)}, bf16[272,256]{1,0:T(8,128)(2,1)S(1)}, u32[]{:S(2)}, u32[]{:S(2)}) collective-permute-start(bf16[272,256]{1,0:T(8,128)(2,1)S(1)} %get-tuple-element.43), channel_id=1, source_target_pairs={{8,12},{9,13},{10,14},{11,15},{24,28},{25,29},{26,30},{27,31}} | collective-permute-start | bytes 417800 | tf_op jit(solution)/shard_map/ppermute | solution.py:382
  44.0 14.8 %copy-start = (bf16[640,2560]{1,0:T(8,128)(2,1)S(1)}, bf16[640,2560]{1,0:T(8,128)(2,1)}, u32[]{:S(2)}) copy-start(bf16[640,2560]{1,0:T(8,128)(2,1)} %refs_1_.1) | copy-start | bytes 9830404
  44.0 14.8 %copy-start.7 = (s32[4]{0:T(128)S(1)}, s32[4]{0:T(128)}, u32[]{:S(2)}) copy-start(s32[4]{0:T(128)} %step_ref.3) | copy-start | bytes 52
  51.9 6.9 %collective-permute-start.17 = (bf16[256,384]{1,0:T(8,128)(2,1)S(1)}, bf16[256,384]{1,0:T(8,128)(2,1)S(1)}, u32[]{:S(2)}, u32[]{:S(2)}) collective-permute-start(bf16[256,384]{1,0:T(8,128)(2,1)S(1)} %join0.1.refs_0_), channel_id=1, source_target_pairs={{0,2},{2,0},{1,3},{3,1},{4,6},{6,4},{5,7},{7,5},{8,10},{10,8},{9,1... | collective-permute-start | bytes 589832 | tf_op jit(solution)/shard_map/ppermute | solution.py:390
  54.4 6.8 %copy-start.6 = (f32[4,2560]{1,0:T(4,128)S(1)}, f32[4,2560]{1,0:T(4,128)}, u32[]{:S(2)}) copy-start(f32[4,2560]{1,0:T(4,128)} %refs_6_.1) | copy-start | bytes 122884
  54.4 6.8 %collective-permute-start.14 = (bf16[256,256]{1,0:T(8,128)(2,1)S(1)}, bf16[256,256]{1,0:T(8,128)(2,1)S(1)}, u32[]{:S(2)}, u32[]{:S(2)}) collective-permute-start(bf16[256,256]{1,0:T(8,128)(2,1)S(1)} %join3.1.refs_1_), channel_id=1, source_target_pairs={{0,2},{2,0},{1,3},{3,1},{4,6},{6,4},{5,7},{7,5},{8,10},{10,8},{9,1... | collective-permute-start | bytes 393224 | tf_op jit(solution)/shard_map/ppermute | solution.py:390
where the time goes:
time: 63.7 us; the launch traced here: 63.3 us
  starting transfers between devices  34.3 us (54%)
  waiting for transfers between devices  12.7 us (20%)
  Pallas kernels  12.2 us (19%)
  local copies, waits for them, and re-layouts  3.61 us (6%)
    ppermute x8, starting transfers between devices, across(): return lax.ppermute(x, 'seq', swap_pairs(cores))  23.6 us
    pallas_call x8, Pallas kernels, call(): pl.pallas_call(kernel, out_shape=out_shape, in_specs=[pl.BlockSpec(memory...  7.96 us
    ppermute x2, waiting for transfers between devices, on_device(): sent = [lax.ppermute(x, 'span', back_up) for x in messages]  7.23 us
    pallas_call x2, Pallas kernels, project(): pl.pallas_call(functools.partial(project_kernel, [(low, own) for _, low,...  4.29 us
    unnamed x16, local copies, waits for them, and re-layouts  3.61 us
    ppermute x2, waiting for transfers between devices, on_device(): theirs = [lax.ppermute(x, 'head', swap_pairs(sides)) for x in mine]  3.31 us
    ppermute x4, starting transfers between devices, up(): lax.ppermute(x, 'span', [(i, i + 1) for i in range(step - 1, spans - 2)])  2.72 us
    ppermute x2, starting transfers between devices, on_device(): sent = [lax.ppermute(x, 'span', back_up) for x in messages]  2.57 us
  transfers between devices with their start and end apart: 18, of which 7 were waited for; matrix products, arithmetic and copies ran while one was open for 0% of the time, Pallas kernels for 16%

commit v1 on v0

--- a/solution.py
+++ b/solution.py
@@ -210,7 +210,7 @@
     return [tuple(out[2 * i : 2 * i + 2]) for i in range(len(roles))]
 
 
-def last_kernel(role, step, groups, mask_ref, ka_ref, kb_ref, va_ref, vb_ref, q_ref, acc_in, top_in, *outs):
+def last_kernel(role, step, groups, mask_ref, ka_ref, kb_low, kb_high, va_ref, vb_ref, q_ref, acc_in, top_in, *outs):
     rows = q_ref.shape[0]
     visible = visible_of(role, step, mask_ref)
 
@@ -226,7 +226,9 @@
         for h in range(q_ref.shape[1] // HD):
             acc, top = acc_in[:, wide(h)], top_in[:, tall(h)]
             if see:
-                keys, values = [ka_ref[:, tall(h)], kb_ref[:, tall(h)]], [va_ref[:, tall(h)], vb_ref[:, tall(h)]]
+                low = h < groups[1][0]
+                other = kb_low[:, tall(h)] if low else kb_high[:, tall(h - groups[1][0])]
+                keys, values = [ka_ref[:, tall(h)], other], [va_ref[:, tall(h)], vb_ref[:, tall(h)]]
                 acc, top = update(q_ref[:, tall(h)], keys, values, acc, top)
             store(h, acc, top)
 
@@ -356,31 +358,30 @@
         w_far = lax.ppermute(out_weight, pair, [(1, 2), (2, 1)])
     asked = lax.ppermute(query_rows, "span", [(spans - 1, spans - 2)])
     query_mate = across(query_rows)
-    if exchange:
-        w_mate = across(out_weight)
-        query_mate = after(query_mate, w_mate)
     queries, lent = [query_rows, query_mate], None
     key, value = key_rows, value_rows
     roles = ["lent", "own"]
     for step in range(final):
         key_next, value_next = up(key, step + 1), up(value, step + 1)
         emit = step + 1 == final
+        keys = [key_next, *(across(key_next[:, a * HD : b * HD]) for a, b in groups)] if emit else [key_next]
         if step == 0:
             (own,), own_draft = attend(block_mask, ["own"], 0, key, value, queries, [], emit)
-            asked = after(asked, own)
+            asked = after(asked, (own, key_next, value_next))
             asks = [asked, across(asked)]
             (lent,), lent_draft = attend(block_mask, ["lent"], 0, key, value, asks, [], emit)
             states, drafts = [lent, own], [*lent_draft, *own_draft]
         else:
-            states, drafts = attend(block_mask, roles, step, key, value, asks + queries, states, emit)
+            waits = [after(asks[0], keys), asks[1], *queries]
+            states, drafts = attend(block_mask, roles, step, key, value, waits, states, emit)
         key, value = key_next, value_next
     lent, own = fold(block_mask, roles, states, [across(x) for x in drafts])
-    keys = [key, across(key)]
     values = [value, across(value)]
     back_up = [(spans - 2, spans - 1)]
     messages = attend_last(block_mask, "lent", final, groups, keys, values, asks[0], lent)
     sent = [lax.ppermute(x, "span", back_up) for x in messages]
     if exchange:
+        w_mate = across(after(out_weight, messages[1]))
         w_back = across(after(w_far, messages[1]))
     own = attend_last(block_mask, "own", final, groups, keys, values, after(query_rows, messages), own)
     mine = [join(block_mask, groups[0], own, sent[0])]

time: 63.7 us -> 63.2 us (level)
  starting transfers between devices: 34.3 us -> 32.2 us
  local copies, waits for them, and re-layouts: 3.61 us -> 4.95 us
    ppermute x8 -> x9, starting transfers between devices: 23.6 us -> 19.2 us  [across(): return lax.ppermute(x, 'seq', swap_pairs(cores))]
    unnamed x16, local copies, waits for them, and re-layouts: 3.61 us -> 4.91 us
    ppermute x1, starting transfers between devices: 2.36 us -> 3.59 us  [on_device(): asked = lax.ppermute(query_rows, 'span', [(spans - 1, spans - 2)])]
    ppermute x2, starting transfers between devices: 2.15 us -> 3.23 us  [on_device(): theirs = [lax.ppermute(x, 'head', swap_pairs(sides)) for x in mine]]
    ppermute x1, waiting for transfers between devices: 0.8 us -> 1.48 us  [on_device(): asked = lax.ppermute(query_rows, 'span', [(spans - 1, spans - 2)])]
    ppermute x8 -> x9, waiting for transfers between devices: 1.38 us -> 1.93 us  [across(): return lax.ppermute(x, 'seq', swap_pairs(cores))]
  transfers between devices with their start and end apart: 18 -> 19, of which waited for: 7 -> 7; matrix products, arithmetic and copies ran while one was open for 0% -> 0% of each run, Pallas kernels for 16% -> 17%
where the time goes in v1:
time: 63.2 us; the launch traced here: 62.5 us
  starting transfers between devices  32.2 us (51%)
  waiting for transfers between devices  12.8 us (20%)
  Pallas kernels  12.2 us (19%)
  local copies, waits for them, and re-layouts  4.95 us (8%)
    ppermute x9, starting transfers between devices, across(): return lax.ppermute(x, 'seq', swap_pairs(cores))  19.2 us
    pallas_call x8, Pallas kernels, call(): pl.pallas_call(kernel, out_shape=out_shape, in_specs=[pl.BlockSpec(memory...  7.95 us
    ppermute x2, waiting for transfers between devices, on_device(): sent = [lax.ppermute(x, 'span', back_up) for x in messages]  6.59 us
    unnamed x16, local copies, waits for them, and re-layouts  4.91 us
    pallas_call x2, Pallas kernels, project(): pl.pallas_call(functools.partial(project_kernel, [(low, own) for _, low,...  4.29 us
    ppermute x1, starting transfers between devices, on_device(): asked = lax.ppermute(query_rows, 'span', [(spans - 1, spans - 2)])  3.59 us
    ppermute x2, starting transfers between devices, on_device(): theirs = [lax.ppermute(x, 'head', swap_pairs(sides)) for x in mine]  3.23 us
    ppermute x2, waiting for transfers between devices, on_device(): theirs = [lax.ppermute(x, 'head', swap_pairs(sides)) for x in mine]  2.75 us
  transfers between devices with their start and end apart: 19, of which 7 were waited for; matrix products, arithmetic and copies ran while one was open for 0% of the time, Pallas kernels for 17%

profile of v1, /device:TPU:28, one launch (start us, length us, event | category | flops | bytes accessed | tf_op | source)
XLA Modules:
  0.0 62.5 jit_solution(15339857190344292938)
XLA Ops:
  0.0 0.9 %collective-permute-start.16 = (bf16[640,2560]{1,0:T(8,128)(2,1)}, bf16[640,2560]{1,0:T(8,128)(2,1)S(1)}, u32[]{:S(2)}, u32[]{:S(2)}) collective-permute-start(bf16[640,2560]{1,0:T(8,128)(2,1)} %refs_1_.1), channel_id=1, source_target_pairs={{1,2},{2,1},{5,6},{6,5},{9,10},{10,9},{13,14},{14,13},{17,18},{18,... | collective-permute-start | bytes 9830408 | tf_op jit(solution)/shard_map/ppermute | solution.py:358
  0.9 0.7 %collective-permute-start = (bf16[256,640]{1,0:T(8,128)(2,1)}, bf16[256,640]{1,0:T(8,128)(2,1)S(1)}, u32[]{:S(2)}, u32[]{:S(2)}) collective-permute-start(bf16[256,640]{1,0:T(8,128)(2,1)} %k_ref.3), channel_id=1, source_target_pairs={{0,4},{4,8},{1,5},{5,9},{2,6},{6,10},{3,7},{7,11},{16,20},{20,24},... | collective-permute-start | bytes 983048 | tf_op jit(solution)/shard_map/ppermute | solution.py:351
  1.6 2.7 %collective-permute-start.8 = (bf16[256,640]{1,0:T(8,128)(2,1)}, bf16[256,640]{1,0:T(8,128)(2,1)S(1)}, u32[]{:S(2)}, u32[]{:S(2)}) collective-permute-start(bf16[256,640]{1,0:T(8,128)(2,1)} %q_ref), channel_id=1, source_target_pairs={{0,1},{1,0},{2,3},{3,2},{4,5},{5,4},{6,7},{7,6},{8,9},{9,8},{10,11... | collective-permute-start | bytes 983048 | tf_op jit(solution)/shard_map/ppermute | solution.py:354
  4.3 0.7 %collective-permute-start.4 = (bf16[256,640]{1,0:T(8,128)(2,1)}, bf16[256,640]{1,0:T(8,128)(2,1)S(1)}, u32[]{:S(2)}, u32[]{:S(2)}) collective-permute-start(bf16[256,640]{1,0:T(8,128)(2,1)} %v_ref.3), channel_id=1, source_target_pairs={{0,4},{4,8},{1,5},{5,9},{2,6},{6,10},{3,7},{7,11},{16,20},{20,24},... | collective-permute-start | bytes 983048 | tf_op jit(solution)/shard_map/ppermute | solution.py:351
  4.9 3.6 %collective-permute-start.7 = (bf16[256,640]{1,0:T(8,128)(2,1)}, bf16[256,640]{1,0:T(8,128)(2,1)S(1)}, u32[]{:S(2)}, u32[]{:S(2)}) collective-permute-start(bf16[256,640]{1,0:T(8,128)(2,1)} %q_ref), channel_id=1, source_target_pairs={{12,8},{13,9},{14,10},{15,11},{28,24},{29,25},{30,26},{31,27}} | collective-permute-start | bytes 983048 | tf_op jit(solution)/shard_map/ppermute | solution.py:359
  8.6 0.7 %collective-permute-start.1 = (bf16[256,640]{1,0:T(8,128)(2,1)S(1)}, bf16[256,640]{1,0:T(8,128)(2,1)S(1)}, u32[]{:S(2)}, u32[]{:S(2)}) collective-permute-start(bf16[256,640]{1,0:T(8,128)(2,1)S(1)} %collective-permute-done.k_ref), channel_id=1, source_target_pairs={{4,8},{5,9},{6,10},{7,11},{20,24},{21,25},{22,26},{23,27}} | collective-permute-start | bytes 983048 | tf_op jit(solution)/shard_map/ppermute | solution.py:351
  9.3 1.0 %copy-done.1 = bf16[256,640]{1,0:T(8,128)(2,1)S(1)} copy-done((bf16[256,640]{1,0:T(8,128)(2,1)S(1)}, bf16[256,640]{1,0:T(8,128)(2,1)}, u32[]{:S(2)}) %copy-start.1) | copy-done | bytes 327704
  10.2 1.0 %copy-done.3 = bf16[256,640]{1,0:T(8,128)(2,1)S(1)} copy-done((bf16[256,640]{1,0:T(8,128)(2,1)S(1)}, bf16[256,640]{1,0:T(8,128)(2,1)}, u32[]{:S(2)}) %copy-start.3) | copy-done | bytes 327704
  11.2 1.0 %copy-done.4 = bf16[256,640]{1,0:T(8,128)(2,1)S(1)} copy-done((bf16[256,640]{1,0:T(8,128)(2,1)S(1)}, bf16[256,640]{1,0:T(8,128)(2,1)}, u32[]{:S(2)}) %copy-start.4) | copy-done | bytes 327704
  12.2 0.7 %copy-done.5 = s32[4,4]{1,0:T(4,128)S(1)} copy-done((s32[4,4]{1,0:T(4,128)S(1)}, s32[4,4]{1,0:T(4,128)}, u32[]{:S(2)}) %copy-start.5) | copy-done | bytes 88
  12.9 1.6 %attend_own0.1 = (f32[512,1280]{1,0:T(8,128)S(1)}, f32[512,640]{1,0:T(8,128)S(1)}) custom-call(s32[4,4]{1,0:T(4,128)S(1)} %copy-done.5, bf16[256,640]{1,0:T(8,128)(2,1)S(1)} %copy-done.3, bf16[256,640]{1,0:T(8,128)(2,1)S(1)} %copy-done.4, bf16[256,640]{1,0:T(8,128)(2,1)S(1)} %copy-done.1, bf16[256,640]{1,0:T(8,128)(2,1)S(1)} %collective-permute-done.8.refs_1_.refs_3_), custom_call_target="tpu_custom_call" | custom-call | flops 1 | bytes 1 | tf_op jit(solution)/shard_map/attend_own0/pallas_call | solution.py:146
  14.5 1.5 %collective-permute-done.7.refs_0_.q_ref = bf16[256,640]{1,0:T(8,128)(2,1)S(1)} collective-permute-done((bf16[256,640]{1,0:T(8,128)(2,1)}, bf16[256,640]{1,0:T(8,128)(2,1)S(1)}, u32[]{:S(2)}, u32[]{:S(2)}) %collective-permute-start.7) | collective-permute-done | bytes 327712 | tf_op jit(solution)/shard_map/ppermute | solution.py:359
  16.0 0.7 %collective-permute-start.5 = (bf16[256,640]{1,0:T(8,128)(2,1)S(1)}, bf16[256,640]{1,0:T(8,128)(2,1)S(1)}, u32[]{:S(2)}, u32[]{:S(2)}) collective-permute-start(bf16[256,640]{1,0:T(8,128)(2,1)S(1)} %collective-permute-done.4.v_ref), channel_id=1, source_target_pairs={{4,8},{5,9},{6,10},{7,11},{20,24},{21,25},{22,26},{23,27}} | collective-permute-start | bytes 983048 | tf_op jit(solution)/shard_map/ppermute | solution.py:351
  16.7 0.6 collective-permute-start.2
  17.6 0.8 %attend_lent0.1 = (f32[512,1280]{1,0:T(8,128)S(1)}, f32[512,640]{1,0:T(8,128)S(1)}) custom-call(s32[4,4]{1,0:T(4,128)S(1)} %copy-done.5, bf16[256,640]{1,0:T(8,128)(2,1)S(1)} %copy-done.3, bf16[256,640]{1,0:T(8,128)(2,1)S(1)} %copy-done.4, bf16[256,640]{1,0:T(8,128)(2,1)S(1)} %collective-permute-done.7.refs_0_.q_ref, ...), custom_call_target="tpu_custom_call" | custom-call | flops 1 | bytes 1 | tf_op jit(solution)/shard_map/attend_lent0/pallas_call | solution.py:146
  18.7 1.1 %attend_lent_own1.1 = (f32[512,1280]{1,0:T(8,128)S(1)}, f32[512,640]{1,0:T(8,128)S(1)}, f32[512,1280]{1,0:T(8,128)S(1)}, f32[512,640]{1,0:T(8,128)S(1)}, bf16[27...) custom-call(s32[4,4]{1,0:T(4,128)S(1)} %copy-done.5, ...), custom_call_target="tpu_custom_call", output_to_operand_aliasing={{0}: (7, {}), {1}: (8, {}), {2}: (9, {}), {3}: (10, {})} | custom-call | flops 1 | bytes 1 | tf_op jit(solution)/shard_map/attend_lent_own1/pallas_call | solution.py:146
  20.5 0.9 %collective-permute-done.10.refs_2_ = bf16[272,640]{1,0:T(8,128)(2,1)S(1)} collective-permute-done((bf16[272,640]{1,0:T(8,128)(2,1)S(1)}, bf16[272,640]{1,0:T(8,128)(2,1)S(1)}, u32[]{:S(2)}, u32[]{:S(2)}) %collective-permute-start.10) | collective-permute-done | bytes 348192 | tf_op jit(solution)/shard_map/ppermute | solution.py:354
  21.9 1.0 %fold.1 = (f32[256,1280]{1,0:T(8,128)S(1)}, f32[256,640]{1,0:T(8,128)S(1)}, f32[256,1280]{1,0:T(8,128)S(1)}, f32[256,640]{1,0:T(8,128)S(1)}) custom-call(s32[4,4]{1,0:T(4,128)S(1)} %copy-done.5, f32[512,1280]{1,0:T(8,128)S(1)} %get-tuple-element.35.refs_0_, f32[512,640]{1,0:T(8,128)S(1)} %get-tuple-element.36.refs_1_, ...), custom_call_target="tpu_custom_call" | custom-call | flops 1 | bytes 1 | tf_op jit(solution)/shard_map/fold/pallas_call | solution.py:146
  23.0 0.6 last_lent.1
  23.6 1.3 %copy-done = bf16[640,2560]{1,0:T(8,128)(2,1)S(1)} copy-done((bf16[640,2560]{1,0:T(8,128)(2,1)S(1)}, bf16[640,2560]{1,0:T(8,128)(2,1)}, u32[]{:S(2)}) %copy-start) | copy-done | bytes 3276824
  25.1 14.9 %collective-permute-start.17 = (bf16[640,2560]{1,0:T(8,128)(2,1)S(1)}, bf16[640,2560]{1,0:T(8,128)(2,1)S(1)}, u32[]{:S(2)}, u32[]{:S(2)}) collective-permute-start(bf16[640,2560]{1,0:T(8,128)(2,1)S(1)} %collective-permute-done.16.refs_5_.refs_3_), channel_id=1, source_target_pairs={{0,1},{1,0},{2,3},{3,2},{4,5},{5,4},{6,7},{7,6},{8,9},{9,8},{10,11... | collective-permute-start | bytes 9830408 | tf_op jit(solution)/shard_map/ppermute | solution.py:354
  40.1 1.3 %collective-permute-start.13 = (bf16[272,384]{1,0:T(8,128)(2,1)S(1)}, bf16[272,384]{1,0:T(8,128)(2,1)S(1)}, u32[]{:S(2)}, u32[]{:S(2)}) collective-permute-start(bf16[272,384]{1,0:T(8,128)(2,1)S(1)} %get-tuple-element.43), channel_id=1, source_target_pairs={{8,12},{9,13},{10,14},{11,15},{24,28},{25,29},{26,30},{27,31}} | collective-permute-start | bytes 626696 | tf_op jit(solution)/shard_map/ppermute | solution.py:382
  41.4 1.3 %collective-permute-start.12 = (bf16[272,256]{1,0:T(8,128)(2,1)S(1)}, bf16[272,256]{1,0:T(8,128)(2,1)S(1)}, u32[]{:S(2)}, u32[]{:S(2)}) collective-permute-start(bf16[272,256]{1,0:T(8,128)(2,1)S(1)} %get-tuple-element.44), channel_id=1, source_target_pairs={{8,12},{9,13},{10,14},{11,15},{24,28},{25,29},{26,30},{27,31}} | collective-permute-start | bytes 417800 | tf_op jit(solution)/shard_map/ppermute | solution.py:382
  42.7 0.7 %last_own.1 = (f32[256,1280]{1,0:T(8,128)S(1)}, f32[256,640]{1,0:T(8,128)S(1)}) custom-call(s32[4,4]{1,0:T(4,128)S(1)} %copy-done.5, bf16[256,640]{1,0:T(8,128)(2,1)S(1)} %collective-permute-done.1.ka_ref, bf16[256,384]{1,0:T(8,128)(2,1)S(1)} %collective-permute-done.2.kb_low, bf16[256,256]{1,0:T(8,128)(2,1)S(1)} %collective-permute-done.3.kb_high, ...), custom_call_target="tpu_custom_call" | custom-call | flops 1 | bytes 1 | tf_op jit(solution)/shard_map/last_own/pallas_call | solution.py:146
  43.4 6.6 %collective-permute-done.13.msg_ref = bf16[272,384]{1,0:T(8,128)(2,1)S(1)} collective-permute-done((bf16[272,384]{1,0:T(8,128)(2,1)S(1)}, bf16[272,384]{1,0:T(8,128)(2,1)S(1)}, u32[]{:S(2)}, u32[]{:S(2)}) %collective-permute-start.13) | collective-permute-done | bytes 208928 | tf_op jit(solution)/shard_map/ppermute | solution.py:382
  50.0 1.0 %join0.1.refs_0_ = bf16[256,384]{1,0:T(8,128)(2,1)S(1)} custom-call(s32[4,4]{1,0:T(4,128)S(1)} %copy-done.5, f32[256,1280]{1,0:T(8,128)S(1)} %get-tuple-element.48.acc_ref, f32[256,640]{1,0:T(8,128)S(1)} %get-tuple-element.49.top_ref, bf16[272,384]{1,0:T(8,128)(2,1)S(1)} %collective-permute-done.13.msg_ref), custom_call_target="tpu_custom_call" | custom-call | flops 1 | bytes 1 | tf_op jit(solution)/shard_map/join0/pallas_call | solution.py:146
  51.0 1.6 %collective-permute-start.18 = (bf16[256,384]{1,0:T(8,128)(2,1)S(1)}, bf16[256,384]{1,0:T(8,128)(2,1)S(1)}, u32[]{:S(2)}, u32[]{:S(2)}) collective-permute-start(bf16[256,384]{1,0:T(8,128)(2,1)S(1)} %join0.1.refs_0_), channel_id=1, source_target_pairs={{0,2},{2,0},{1,3},{3,1},{4,6},{6,4},{5,7},{7,5},{8,10},{10,8},{9,1... | collective-permute-start | bytes 589832 | tf_op jit(solution)/shard_map/ppermute | solution.py:391
  52.6 1.1 %join3.1.refs_1_ = bf16[256,256]{1,0:T(8,128)(2,1)S(1)} custom-call(s32[4,4]{1,0:T(4,128)S(1)} %copy-done.5, f32[256,1280]{1,0:T(8,128)S(1)} %get-tuple-element.48.acc_ref, f32[256,640]{1,0:T(8,128)S(1)} %get-tuple-element.49.top_ref, bf16[272,256]{1,0:T(8,128)(2,1)S(1)} %collective-permute-done.12.msg_ref), custom_call_target="tpu_custom_call" | custom-call | flops 1 | bytes 1 | tf_op jit(solution)/shard_map/join3/pallas_call | solution.py:146
  53.7 1.6 %collective-permute-start.14 = (bf16[256,256]{1,0:T(8,128)(2,1)S(1)}, bf16[256,256]{1,0:T(8,128)(2,1)S(1)}, u32[]{:S(2)}, u32[]{:S(2)}) collective-permute-start(bf16[256,256]{1,0:T(8,128)(2,1)S(1)} %join3.1.refs_1_), channel_id=1, source_target_pairs={{0,2},{2,0},{1,3},{3,1},{4,6},{6,4},{5,7},{7,5},{8,10},{10,8},{9,1... | collective-permute-start | bytes 393224 | tf_op jit(solution)/shard_map/ppermute | solution.py:391
  55.3 2.8 %collective-permute-done.18.refs_2_ = bf16[256,384]{1,0:T(8,128)(2,1)S(1)} collective-permute-done((bf16[256,384]{1,0:T(8,128)(2,1)S(1)}, bf16[256,384]{1,0:T(8,128)(2,1)S(1)}, u32[]{:S(2)}, u32[]{:S(2)}) %collective-permute-start.18) | collective-permute-done | bytes 196640 | tf_op jit(solution)/shard_map/ppermute | solution.py:391
  58.1 2.4 %project_most.1.refs_5_ = f32[256,2560]{1,0:T(8,128)S(1)} custom-call(s32[4]{0:T(128)S(1)} %copy-done.7, bf16[256,384]{1,0:T(8,128)(2,1)S(1)} %join0.1.refs_0_, bf16[256,256]{1,0:T(8,128)(2,1)S(1)} %join3.1.refs_1_, bf16[256,384]{1,0:T(8,128)(2,1)S(1)} %collective-permute-done.18.refs_2_, bf16[640,2560]{1,0:T(8,128)(2,1)S(1)} %copy-done, ...), custom_call_target="tpu_custom_call" | custom-call | flops 1 | bytes 1 | tf_op jit(solution)/shard_map/project_most/pallas_call | solution.py:316
  60.5 1.9 %project_last.1 = bf16[256,2560]{1,0:T(8,128)(2,1)} custom-call(s32[4]{0:T(128)S(1)} %copy-done.7, bf16[256,256]{1,0:T(8,128)(2,1)S(1)} %collective-permute-done.14.refs_0_, bf16[640,2560]{1,0:T(8,128)(2,1)S(1)} %copy-done, bf16[640,2560]{1,0:T(8,128)(2,1)S(1)} %collective-permute-done.15.refs_4_.refs_2_, ...), custom_call_target="tpu_custom_call" | custom-call | flops 1 | bytes 1 | tf_op jit(solution)/shard_map/project_last/pallas_call | solution.py:316
  (34 shorter events, 2.1 us)
Async XLA Ops:
  0.0 25.1 %collective-permute-start.16 = (bf16[640,2560]{1,0:T(8,128)(2,1)}, bf16[640,2560]{1,0:T(8,128)(2,1)S(1)}, u32[]{:S(2)}, u32[]{:S(2)}) collective-permute-start(bf16[640,2560]{1,0:T(8,128)(2,1)} %refs_1_.1), channel_id=1, source_target_pairs={{1,2},{2,1},{5,6},{6,5},{9,10},{10,9},{13,14},{14,13},{17,18},{18,... | collective-permute-start | bytes 9830408 | tf_op jit(solution)/shard_map/ppermute | solution.py:358
  0.9 7.7 %collective-permute-start = (bf16[256,640]{1,0:T(8,128)(2,1)}, bf16[256,640]{1,0:T(8,128)(2,1)S(1)}, u32[]{:S(2)}, u32[]{:S(2)}) collective-permute-start(bf16[256,640]{1,0:T(8,128)(2,1)} %k_ref.3), channel_id=1, source_target_pairs={{0,4},{4,8},{1,5},{5,9},{2,6},{6,10},{3,7},{7,11},{16,20},{20,24},... | collective-permute-start | bytes 983048 | tf_op jit(solution)/shard_map/ppermute | solution.py:351
  1.6 7.7 %collective-permute-start.8 = (bf16[256,640]{1,0:T(8,128)(2,1)}, bf16[256,640]{1,0:T(8,128)(2,1)S(1)}, u32[]{:S(2)}, u32[]{:S(2)}) collective-permute-start(bf16[256,640]{1,0:T(8,128)(2,1)} %q_ref), channel_id=1, source_target_pairs={{0,1},{1,0},{2,3},{3,2},{4,5},{5,4},{6,7},{7,6},{8,9},{9,8},{10,11... | collective-permute-start | bytes 983048 | tf_op jit(solution)/shard_map/ppermute | solution.py:354
  4.3 10.2 %collective-permute-start.4 = (bf16[256,640]{1,0:T(8,128)(2,1)}, bf16[256,640]{1,0:T(8,128)(2,1)S(1)}, u32[]{:S(2)}, u32[]{:S(2)}) collective-permute-start(bf16[256,640]{1,0:T(8,128)(2,1)} %v_ref.3), channel_id=1, source_target_pairs={{0,4},{4,8},{1,5},{5,9},{2,6},{6,10},{3,7},{7,11},{16,20},{20,24},... | collective-permute-start | bytes 983048 | tf_op jit(solution)/shard_map/ppermute | solution.py:351
  4.9 11.0 %collective-permute-start.7 = (bf16[256,640]{1,0:T(8,128)(2,1)}, bf16[256,640]{1,0:T(8,128)(2,1)S(1)}, u32[]{:S(2)}, u32[]{:S(2)}) collective-permute-start(bf16[256,640]{1,0:T(8,128)(2,1)} %q_ref), channel_id=1, source_target_pairs={{12,8},{13,9},{14,10},{15,11},{28,24},{29,25},{30,26},{31,27}} | collective-permute-start | bytes 983048 | tf_op jit(solution)/shard_map/ppermute | solution.py:359
  8.6 8.1 %collective-permute-start.1 = (bf16[256,640]{1,0:T(8,128)(2,1)S(1)}, bf16[256,640]{1,0:T(8,128)(2,1)S(1)}, u32[]{:S(2)}, u32[]{:S(2)}) collective-permute-start(bf16[256,640]{1,0:T(8,128)(2,1)S(1)} %collective-permute-done.k_ref), channel_id=1, source_target_pairs={{4,8},{5,9},{6,10},{7,11},{20,24},{21,25},{22,26},{23,27}} | collective-permute-start | bytes 983048 | tf_op jit(solution)/shard_map/ppermute | solution.py:351
  9.3 1.0 %copy-start.1 = (bf16[256,640]{1,0:T(8,128)(2,1)S(1)}, bf16[256,640]{1,0:T(8,128)(2,1)}, u32[]{:S(2)}) copy-start(bf16[256,640]{1,0:T(8,128)(2,1)} %q_ref) | copy-start | bytes 983044
  10.2 1.0 %copy-start.3 = (bf16[256,640]{1,0:T(8,128)(2,1)S(1)}, bf16[256,640]{1,0:T(8,128)(2,1)}, u32[]{:S(2)}) copy-start(bf16[256,640]{1,0:T(8,128)(2,1)} %k_ref.3) | copy-start | bytes 983044
  11.2 1.0 %copy-start.4 = (bf16[256,640]{1,0:T(8,128)(2,1)S(1)}, bf16[256,640]{1,0:T(8,128)(2,1)}, u32[]{:S(2)}) copy-start(bf16[256,640]{1,0:T(8,128)(2,1)} %v_ref.3) | copy-start | bytes 983044
  12.2 0.7 %copy-start.5 = (s32[4,4]{1,0:T(4,128)S(1)}, s32[4,4]{1,0:T(4,128)}, u32[]{:S(2)}) copy-start(s32[4,4]{1,0:T(4,128)} %mask_ref.15) | copy-start | bytes 196
  12.9 5.8 %copy-start.2 = (bf16[256,640]{1,0:T(8,128)(2,1)S(1)}, bf16[256,640]{1,0:T(8,128)(2,1)}, u32[]{:S(2)}) copy-start(bf16[256,640]{1,0:T(8,128)(2,1)} %q_ref) | copy-start | bytes 983044
  16.0 1.6 %collective-permute-start.9 = (bf16[256,640]{1,0:T(8,128)(2,1)S(1)}, bf16[256,640]{1,0:T(8,128)(2,1)S(1)}, u32[]{:S(2)}, u32[]{:S(2)}) collective-permute-start(bf16[256,640]{1,0:T(8,128)(2,1)S(1)} %collective-permute-done.7.refs_0_.q_ref), channel_id=1, source_target_pairs={{0,1},{1,0},{2,3},{3,2},{4,5},{5,4},{6,7},{7,6},{8,9},{9,8},{10,11... | collective-permute-start | bytes 983048 | tf_op jit(solution)/shard_map/ppermute | solution.py:354
  16.0 4.3 %collective-permute-start.5 = (bf16[256,640]{1,0:T(8,128)(2,1)S(1)}, bf16[256,640]{1,0:T(8,128)(2,1)S(1)}, u32[]{:S(2)}, u32[]{:S(2)}) collective-permute-start(bf16[256,640]{1,0:T(8,128)(2,1)S(1)} %collective-permute-done.4.v_ref), channel_id=1, source_target_pairs={{4,8},{5,9},{6,10},{7,11},{20,24},{21,25},{22,26},{23,27}} | collective-permute-start | bytes 983048 | tf_op jit(solution)/shard_map/ppermute | solution.py:351
  16.7 2.0 %collective-permute-start.2 = (bf16[256,384]{1,0:T(8,128)(2,1)S(1)}, bf16[256,384]{1,0:T(8,128)(2,1)S(1)}, u32[]{:S(2)}, u32[]{:S(2)}) collective-permute-start(bf16[256,384]{1,0:T(8,128)(2,1)S(1)} %slice.8), channel_id=1, source_target_pairs={{0,1},{1,0},{2,3},{3,2},{4,5},{5,4},{6,7},{7,6},{8,9},{9,8},{10,11... | collective-permute-start | bytes 589832 | tf_op jit(solution)/shard_map/ppermute | solution.py:354
  17.3 1.4 %collective-permute-start.3 = (bf16[256,256]{1,0:T(8,128)(2,1)S(1)}, bf16[256,256]{1,0:T(8,128)(2,1)S(1)}, u32[]{:S(2)}, u32[]{:S(2)}) collective-permute-start(bf16[256,256]{1,0:T(8,128)(2,1)S(1)} %slice.9), channel_id=1, source_target_pairs={{0,1},{1,0},{2,3},{3,2},{4,5},{5,4},{6,7},{7,6},{8,9},{9,8},{10,11... | collective-permute-start | bytes 393224 | tf_op jit(solution)/shard_map/ppermute | solution.py:354
  19.8 1.7 %collective-permute-start.10 = (bf16[272,640]{1,0:T(8,128)(2,1)S(1)}, bf16[272,640]{1,0:T(8,128)(2,1)S(1)}, u32[]{:S(2)}, u32[]{:S(2)}) collective-permute-start(bf16[272,640]{1,0:T(8,128)(2,1)S(1)} %get-tuple-element.37), channel_id=1, source_target_pairs={{0,1},{1,0},{2,3},{3,2},{4,5},{5,4},{6,7},{7,6},{8,9},{9,8},{10,11... | collective-permute-start | bytes 1044488 | tf_op jit(solution)/shard_map/ppermute | solution.py:354
  20.0 2.0 %collective-permute-start.11 = (bf16[272,640]{1,0:T(8,128)(2,1)S(1)}, bf16[272,640]{1,0:T(8,128)(2,1)S(1)}, u32[]{:S(2)}, u32[]{:S(2)}) collective-permute-start(bf16[272,640]{1,0:T(8,128)(2,1)S(1)} %get-tuple-element.40), channel_id=1, source_target_pairs={{0,1},{1,0},{2,3},{3,2},{4,5},{5,4},{6,7},{7,6},{8,9},{9,8},{10,11... | collective-permute-start | bytes 1044488 | tf_op jit(solution)/shard_map/ppermute | solution.py:354
  20.3 2.7 %collective-permute-start.6 = (bf16[256,640]{1,0:T(8,128)(2,1)S(1)}, bf16[256,640]{1,0:T(8,128)(2,1)S(1)}, u32[]{:S(2)}, u32[]{:S(2)}) collective-permute-start(bf16[256,640]{1,0:T(8,128)(2,1)S(1)} %collective-permute-done.5.va_ref), channel_id=1, source_target_pairs={{0,1},{1,0},{2,3},{3,2},{4,5},{5,4},{6,7},{7,6},{8,9},{9,8},{10,11... | collective-permute-start | bytes 983048 | tf_op jit(solution)/shard_map/ppermute | solution.py:354
  23.0 1.9 %copy-start = (bf16[640,2560]{1,0:T(8,128)(2,1)S(1)}, bf16[640,2560]{1,0:T(8,128)(2,1)}, u32[]{:S(2)}) copy-start(bf16[640,2560]{1,0:T(8,128)(2,1)} %refs_1_.1) | copy-start | bytes 9830404
  24.9 33.1 %collective-permute-start.15 = (bf16[640,2560]{1,0:T(8,128)(2,1)S(1)}, bf16[640,2560]{1,0:T(8,128)(2,1)S(1)}, u32[]{:S(2)}, u32[]{:S(2)}) collective-permute-start(bf16[640,2560]{1,0:T(8,128)(2,1)S(1)} %copy-done), channel_id=1, source_target_pairs={{0,1},{1,0},{2,3},{3,2},{4,5},{5,4},{6,7},{7,6},{8,9},{9,8},{10,11... | collective-permute-start | bytes 9830408 | tf_op jit(solution)/shard_map/ppermute | solution.py:354
  25.1 32.9 %collective-permute-start.17 = (bf16[640,2560]{1,0:T(8,128)(2,1)S(1)}, bf16[640,2560]{1,0:T(8,128)(2,1)S(1)}, u32[]{:S(2)}, u32[]{:S(2)}) collective-permute-start(bf16[640,2560]{1,0:T(8,128)(2,1)S(1)} %collective-permute-done.16.refs_5_.refs_3_), channel_id=1, source_target_pairs={{0,1},{1,0},{2,3},{3,2},{4,5},{5,4},{6,7},{7,6},{8,9},{9,8},{10,11... | collective-permute-start | bytes 9830408 | tf_op jit(solution)/shard_map/ppermute | solution.py:354
  40.1 9.9 %collective-permute-start.13 = (bf16[272,384]{1,0:T(8,128)(2,1)S(1)}, bf16[272,384]{1,0:T(8,128)(2,1)S(1)}, u32[]{:S(2)}, u32[]{:S(2)}) collective-permute-start(bf16[272,384]{1,0:T(8,128)(2,1)S(1)} %get-tuple-element.43), channel_id=1, source_target_pairs={{8,12},{9,13},{10,14},{11,15},{24,28},{25,29},{26,30},{27,31}} | collective-permute-start | bytes 626696 | tf_op jit(solution)/shard_map/ppermute | solution.py:382
  41.4 11.2 %collective-permute-start.12 = (bf16[272,256]{1,0:T(8,128)(2,1)S(1)}, bf16[272,256]{1,0:T(8,128)(2,1)S(1)}, u32[]{:S(2)}, u32[]{:S(2)}) collective-permute-start(bf16[272,256]{1,0:T(8,128)(2,1)S(1)} %get-tuple-element.44), channel_id=1, source_target_pairs={{8,12},{9,13},{10,14},{11,15},{24,28},{25,29},{26,30},{27,31}} | collective-permute-start | bytes 417800 | tf_op jit(solution)/shard_map/ppermute | solution.py:382
  43.4 14.7 %copy-start.7 = (s32[4]{0:T(128)S(1)}, s32[4]{0:T(128)}, u32[]{:S(2)}) copy-start(s32[4]{0:T(128)} %step_ref.3) | copy-start | bytes 52
  51.0 7.1 %collective-permute-start.18 = (bf16[256,384]{1,0:T(8,128)(2,1)S(1)}, bf16[256,384]{1,0:T(8,128)(2,1)S(1)}, u32[]{:S(2)}, u32[]{:S(2)}) collective-permute-start(bf16[256,384]{1,0:T(8,128)(2,1)S(1)} %join0.1.refs_0_), channel_id=1, source_target_pairs={{0,2},{2,0},{1,3},{3,1},{4,6},{6,4},{5,7},{7,5},{8,10},{10,8},{9,1... | collective-permute-start | bytes 589832 | tf_op jit(solution)/shard_map/ppermute | solution.py:391
  53.7 6.8 %copy-start.6 = (f32[4,2560]{1,0:T(4,128)S(1)}, f32[4,2560]{1,0:T(4,128)}, u32[]{:S(2)}) copy-start(f32[4,2560]{1,0:T(4,128)} %refs_6_.1) | copy-start | bytes 122884
  53.7 6.8 %collective-permute-start.14 = (bf16[256,256]{1,0:T(8,128)(2,1)S(1)}, bf16[256,256]{1,0:T(8,128)(2,1)S(1)}, u32[]{:S(2)}, u32[]{:S(2)}) collective-permute-start(bf16[256,256]{1,0:T(8,128)(2,1)S(1)} %join3.1.refs_1_), channel_id=1, source_target_pairs={{0,2},{2,0},{1,3},{3,1},{4,6},{6,4},{5,7},{7,5},{8,10},{10,8},{9,1... | collective-permute-start | bytes 393224 | tf_op jit(solution)/shard_map/ppermute | solution.py:391

commit v2 on v1

--- a/solution.py
+++ b/solution.py
@@ -277,12 +277,13 @@
     count = len(lows)
     rows_refs, (w_own, w_mate, w_far, w_back), refs = refs[:count], refs[count : count + 4], refs[count + 4 :]
     straight = lax.axis_index("head") == lax.axis_index("seq")
-    last = len(refs) > 1
+    last, added = len(refs) > 2, len(refs) > 1
+    total_ref = refs[0] if added else None
     if last:
         total_ref, gate_ref, out_ref, stage, sems = refs
         gate_row = pl.ds(step_ref[lax.axis_index("span")], 1)
     else:
-        out_ref = refs[0]
+        out_ref = refs[-1]
     tiles = out_ref.shape[1] // TILE
 
     def copy(t):
@@ -291,7 +292,7 @@
     def run(w_mine, w_theirs):
         for t in range(tiles):
             lanes = slice(t * TILE, (t + 1) * TILE)
-            total = total_ref[:, lanes] if last else None
+            total = total_ref[:, lanes] if added else None
             for ref, (low, own) in zip(rows_refs, lows):
                 weight = w_mine if own else w_theirs
                 term = dot(ref[...], weight[low : low + ref.shape[1], lanes], ((1,), (0,)))
@@ -311,8 +312,8 @@
 
 def project(step_index, terms, weights, total=None, gate_table=None):
     rows, columns = terms[0][0].shape[0], weights[0].shape[1]
-    last = total is not None
-    operands = [x for x, _, _ in terms] + [*weights] + ([total, gate_table] if last else [])
+    last = gate_table is not None
+    operands = [x for x, _, _ in terms] + [*weights] + [x for x in (total, gate_table) if x is not None]
     return pl.pallas_call(
         functools.partial(project_kernel, [(low, own) for _, low, own in terms]),
         out_shape=jax.ShapeDtypeStruct((rows, columns), jnp.bfloat16 if last else jnp.float32),
@@ -327,7 +328,7 @@
         else [],
         compiler_params=pltpu.CompilerParams(vmem_limit_bytes=VMEM_LIMIT),
         cost_estimate=BRIEF,
-        name="project_last" if last else "project_most",
+        name="project_last" if last else "project_most" if total is None else "project_more",
     )(step_index, *operands)
 
 
@@ -390,8 +391,8 @@
     if exchange:
         theirs = [lax.ppermute(x, "head", swap_pairs(sides)) for x in mine]
         weights, low = [out_weight, w_mate, w_far, w_back], split * HD
-        most = [(mine[0], 0, True), (mine[1], low, True), (theirs[0], 0, False)]
-        total = project(step_index, most, weights)
+        total = project(step_index, [(mine[0], 0, True), (mine[1], low, True)], weights)
+        total = project(step_index, [(theirs[0], 0, False)], weights, total)
         return project(step_index, [(theirs[1], low, False)], weights, total, gate_table)
     weight = lax.all_gather(out_weight, "seq", axis=1, tiled=True)
     projected = jnp.dot(jnp.concatenate(mine, axis=1), weight, preferred_element_type=jnp.float32)

time: 63.2 us -> 62.5 us (0.989)
  waiting for transfers between devices: 12.8 us -> 11.4 us
  Pallas kernels: 12.2 us -> 13 us
    ppermute x2, waiting for transfers between devices: 2.75 us -> 1.34 us  [on_device(): theirs = [lax.ppermute(x, 'head', swap_pairs(sides)) for x in mine]]
    pallas_call x2 -> x3, Pallas kernels: 4.29 us -> 5 us  [project(): pl.pallas_call(functools.partial(project_kernel, [(low, own) for _, low,...]
  transfers between devices with their start and end apart: 19 -> 19, of which waited for: 7 -> 8; matrix products, arithmetic and copies ran while one was open for 0% -> 0% of each run, Pallas kernels for 17% -> 18%
where the time goes in v2:
time: 62.5 us; the launch traced here: 61.8 us
  starting transfers between devices  32.2 us (52%)
  Pallas kernels  13 us (21%)
  waiting for transfers between devices  11.4 us (18%)
  local copies, waits for them, and re-layouts  4.95 us (8%)
    ppermute x9, starting transfers between devices, across(): return lax.ppermute(x, 'seq', swap_pairs(cores))  19.2 us
    pallas_call x8, Pallas kernels, call(): pl.pallas_call(kernel, out_shape=out_shape, in_specs=[pl.BlockSpec(memory...  7.96 us
    ppermute x2, waiting for transfers between devices, on_device(): sent = [lax.ppermute(x, 'span', back_up) for x in messages]  6.59 us
    pallas_call x3, Pallas kernels, project(): pl.pallas_call(functools.partial(project_kernel, [(low, own) for _, low,...  5 us
    unnamed x16, local copies, waits for them, and re-layouts  4.91 us
    ppermute x1, starting transfers between devices, on_device(): asked = lax.ppermute(query_rows, 'span', [(spans - 1, spans - 2)])  3.59 us
    ppermute x2, starting transfers between devices, on_device(): theirs = [lax.ppermute(x, 'head', swap_pairs(sides)) for x in mine]  3.23 us
    ppermute x4, starting transfers between devices, up(): lax.ppermute(x, 'span', [(i, i + 1) for i in range(step - 1, spans - 2)])  2.7 us
  transfers between devices with their start and end apart: 19, of which 8 were waited for; matrix products, arithmetic and copies ran while one was open for 0% of the time, Pallas kernels for 18%

profile of v2, /device:TPU:28, one launch (start us, length us, event | category | flops | bytes accessed | tf_op | source)
XLA Modules:
  0.0 61.8 jit_solution(10401105510578107503)
XLA Ops:
  0.0 0.9 %collective-permute-start.16 = (bf16[640,2560]{1,0:T(8,128)(2,1)}, bf16[640,2560]{1,0:T(8,128)(2,1)S(1)}, u32[]{:S(2)}, u32[]{:S(2)}) collective-permute-start(bf16[640,2560]{1,0:T(8,128)(2,1)} %refs_1_.3), channel_id=1, source_target_pairs={{1,2},{2,1},{5,6},{6,5},{9,10},{10,9},{13,14},{14,13},{17,18},{18,... | collective-permute-start | bytes 9830408 | tf_op jit(solution)/shard_map/ppermute | solution.py:359
  0.9 0.7 %collective-permute-start = (bf16[256,640]{1,0:T(8,128)(2,1)}, bf16[256,640]{1,0:T(8,128)(2,1)S(1)}, u32[]{:S(2)}, u32[]{:S(2)}) collective-permute-start(bf16[256,640]{1,0:T(8,128)(2,1)} %k_ref.3), channel_id=1, source_target_pairs={{0,4},{4,8},{1,5},{5,9},{2,6},{6,10},{3,7},{7,11},{16,20},{20,24},... | collective-permute-start | bytes 983048 | tf_op jit(solution)/shard_map/ppermute | solution.py:352
  1.6 2.7 %collective-permute-start.8 = (bf16[256,640]{1,0:T(8,128)(2,1)}, bf16[256,640]{1,0:T(8,128)(2,1)S(1)}, u32[]{:S(2)}, u32[]{:S(2)}) collective-permute-start(bf16[256,640]{1,0:T(8,128)(2,1)} %q_ref), channel_id=1, source_target_pairs={{0,1},{1,0},{2,3},{3,2},{4,5},{5,4},{6,7},{7,6},{8,9},{9,8},{10,11... | collective-permute-start | bytes 983048 | tf_op jit(solution)/shard_map/ppermute | solution.py:355
  4.3 0.7 %collective-permute-start.4 = (bf16[256,640]{1,0:T(8,128)(2,1)}, bf16[256,640]{1,0:T(8,128)(2,1)S(1)}, u32[]{:S(2)}, u32[]{:S(2)}) collective-permute-start(bf16[256,640]{1,0:T(8,128)(2,1)} %v_ref.3), channel_id=1, source_target_pairs={{0,4},{4,8},{1,5},{5,9},{2,6},{6,10},{3,7},{7,11},{16,20},{20,24},... | collective-permute-start | bytes 983048 | tf_op jit(solution)/shard_map/ppermute | solution.py:352
  4.9 3.6 %collective-permute-start.7 = (bf16[256,640]{1,0:T(8,128)(2,1)}, bf16[256,640]{1,0:T(8,128)(2,1)S(1)}, u32[]{:S(2)}, u32[]{:S(2)}) collective-permute-start(bf16[256,640]{1,0:T(8,128)(2,1)} %q_ref), channel_id=1, source_target_pairs={{12,8},{13,9},{14,10},{15,11},{28,24},{29,25},{30,26},{31,27}} | collective-permute-start | bytes 983048 | tf_op jit(solution)/shard_map/ppermute | solution.py:360
  8.6 0.7 %collective-permute-start.1 = (bf16[256,640]{1,0:T(8,128)(2,1)S(1)}, bf16[256,640]{1,0:T(8,128)(2,1)S(1)}, u32[]{:S(2)}, u32[]{:S(2)}) collective-permute-start(bf16[256,640]{1,0:T(8,128)(2,1)S(1)} %collective-permute-done.k_ref), channel_id=1, source_target_pairs={{4,8},{5,9},{6,10},{7,11},{20,24},{21,25},{22,26},{23,27}} | collective-permute-start | bytes 983048 | tf_op jit(solution)/shard_map/ppermute | solution.py:352
  9.3 1.0 %copy-done.1 = bf16[256,640]{1,0:T(8,128)(2,1)S(1)} copy-done((bf16[256,640]{1,0:T(8,128)(2,1)S(1)}, bf16[256,640]{1,0:T(8,128)(2,1)}, u32[]{:S(2)}) %copy-start.1) | copy-done | bytes 327704
  10.2 1.0 %copy-done.3 = bf16[256,640]{1,0:T(8,128)(2,1)S(1)} copy-done((bf16[256,640]{1,0:T(8,128)(2,1)S(1)}, bf16[256,640]{1,0:T(8,128)(2,1)}, u32[]{:S(2)}) %copy-start.3) | copy-done | bytes 327704
  11.2 1.0 %copy-done.4 = bf16[256,640]{1,0:T(8,128)(2,1)S(1)} copy-done((bf16[256,640]{1,0:T(8,128)(2,1)S(1)}, bf16[256,640]{1,0:T(8,128)(2,1)}, u32[]{:S(2)}) %copy-start.4) | copy-done | bytes 327704
  12.2 0.7 %copy-done.5 = s32[4,4]{1,0:T(4,128)S(1)} copy-done((s32[4,4]{1,0:T(4,128)S(1)}, s32[4,4]{1,0:T(4,128)}, u32[]{:S(2)}) %copy-start.5) | copy-done | bytes 88
  12.9 1.6 %attend_own0.1 = (f32[512,1280]{1,0:T(8,128)S(1)}, f32[512,640]{1,0:T(8,128)S(1)}) custom-call(s32[4,4]{1,0:T(4,128)S(1)} %copy-done.5, bf16[256,640]{1,0:T(8,128)(2,1)S(1)} %copy-done.3, bf16[256,640]{1,0:T(8,128)(2,1)S(1)} %copy-done.4, bf16[256,640]{1,0:T(8,128)(2,1)S(1)} %copy-done.1, bf16[256,640]{1,0:T(8,128)(2,1)S(1)} %collective-permute-done.8.refs_1_.refs_3_), custom_call_target="tpu_custom_call" | custom-call | flops 1 | bytes 1 | tf_op jit(solution)/shard_map/attend_own0/pallas_call | solution.py:146
  14.5 1.5 %collective-permute-done.7.refs_0_.q_ref = bf16[256,640]{1,0:T(8,128)(2,1)S(1)} collective-permute-done((bf16[256,640]{1,0:T(8,128)(2,1)}, bf16[256,640]{1,0:T(8,128)(2,1)S(1)}, u32[]{:S(2)}, u32[]{:S(2)}) %collective-permute-start.7) | collective-permute-done | bytes 327712 | tf_op jit(solution)/shard_map/ppermute | solution.py:360
  16.0 0.7 %collective-permute-start.5 = (bf16[256,640]{1,0:T(8,128)(2,1)S(1)}, bf16[256,640]{1,0:T(8,128)(2,1)S(1)}, u32[]{:S(2)}, u32[]{:S(2)}) collective-permute-start(bf16[256,640]{1,0:T(8,128)(2,1)S(1)} %collective-permute-done.4.v_ref), channel_id=1, source_target_pairs={{4,8},{5,9},{6,10},{7,11},{20,24},{21,25},{22,26},{23,27}} | collective-permute-start | bytes 983048 | tf_op jit(solution)/shard_map/ppermute | solution.py:352
  17.6 0.8 %attend_lent0.1 = (f32[512,1280]{1,0:T(8,128)S(1)}, f32[512,640]{1,0:T(8,128)S(1)}) custom-call(s32[4,4]{1,0:T(4,128)S(1)} %copy-done.5, bf16[256,640]{1,0:T(8,128)(2,1)S(1)} %copy-done.3, bf16[256,640]{1,0:T(8,128)(2,1)S(1)} %copy-done.4, bf16[256,640]{1,0:T(8,128)(2,1)S(1)} %collective-permute-done.7.refs_0_.q_ref, ...), custom_call_target="tpu_custom_call" | custom-call | flops 1 | bytes 1 | tf_op jit(solution)/shard_map/attend_lent0/pallas_call | solution.py:146
  18.7 1.1 %attend_lent_own1.1 = (f32[512,1280]{1,0:T(8,128)S(1)}, f32[512,640]{1,0:T(8,128)S(1)}, f32[512,1280]{1,0:T(8,128)S(1)}, f32[512,640]{1,0:T(8,128)S(1)}, bf16[27...) custom-call(s32[4,4]{1,0:T(4,128)S(1)} %copy-done.5, ...), custom_call_target="tpu_custom_call", output_to_operand_aliasing={{0}: (7, {}), {1}: (8, {}), {2}: (9, {}), {3}: (10, {})} | custom-call | flops 1 | bytes 1 | tf_op jit(solution)/shard_map/attend_lent_own1/pallas_call | solution.py:146
  20.5 0.9 %collective-permute-done.10.refs_2_ = bf16[272,640]{1,0:T(8,128)(2,1)S(1)} collective-permute-done((bf16[272,640]{1,0:T(8,128)(2,1)S(1)}, bf16[272,640]{1,0:T(8,128)(2,1)S(1)}, u32[]{:S(2)}, u32[]{:S(2)}) %collective-permute-start.10) | collective-permute-done | bytes 348192 | tf_op jit(solution)/shard_map/ppermute | solution.py:355
  21.9 1.1 %fold.1 = (f32[256,1280]{1,0:T(8,128)S(1)}, f32[256,640]{1,0:T(8,128)S(1)}, f32[256,1280]{1,0:T(8,128)S(1)}, f32[256,640]{1,0:T(8,128)S(1)}) custom-call(s32[4,4]{1,0:T(4,128)S(1)} %copy-done.5, f32[512,1280]{1,0:T(8,128)S(1)} %get-tuple-element.35.refs_0_, f32[512,640]{1,0:T(8,128)S(1)} %get-tuple-element.36.refs_1_, ...), custom_call_target="tpu_custom_call" | custom-call | flops 1 | bytes 1 | tf_op jit(solution)/shard_map/fold/pallas_call | solution.py:146
  23.0 0.6 last_lent.1
  23.6 1.3 %copy-done = bf16[640,2560]{1,0:T(8,128)(2,1)S(1)} copy-done((bf16[640,2560]{1,0:T(8,128)(2,1)S(1)}, bf16[640,2560]{1,0:T(8,128)(2,1)}, u32[]{:S(2)}) %copy-start) | copy-done | bytes 3276824
  25.1 14.9 %collective-permute-start.17 = (bf16[640,2560]{1,0:T(8,128)(2,1)S(1)}, bf16[640,2560]{1,0:T(8,128)(2,1)S(1)}, u32[]{:S(2)}, u32[]{:S(2)}) collective-permute-start(bf16[640,2560]{1,0:T(8,128)(2,1)S(1)} %collective-permute-done.16.refs_4_.refs_3_), channel_id=1, source_target_pairs={{0,1},{1,0},{2,3},{3,2},{4,5},{5,4},{6,7},{7,6},{8,9},{9,8},{10,11... | collective-permute-start | bytes 9830408 | tf_op jit(solution)/shard_map/ppermute | solution.py:355
  40.1 1.3 %collective-permute-start.13 = (bf16[272,384]{1,0:T(8,128)(2,1)S(1)}, bf16[272,384]{1,0:T(8,128)(2,1)S(1)}, u32[]{:S(2)}, u32[]{:S(2)}) collective-permute-start(bf16[272,384]{1,0:T(8,128)(2,1)S(1)} %get-tuple-element.43), channel_id=1, source_target_pairs={{8,12},{9,13},{10,14},{11,15},{24,28},{25,29},{26,30},{27,31}} | collective-permute-start | bytes 626696 | tf_op jit(solution)/shard_map/ppermute | solution.py:383
  41.4 1.3 %collective-permute-start.12 = (bf16[272,256]{1,0:T(8,128)(2,1)S(1)}, bf16[272,256]{1,0:T(8,128)(2,1)S(1)}, u32[]{:S(2)}, u32[]{:S(2)}) collective-permute-start(bf16[272,256]{1,0:T(8,128)(2,1)S(1)} %get-tuple-element.44), channel_id=1, source_target_pairs={{8,12},{9,13},{10,14},{11,15},{24,28},{25,29},{26,30},{27,31}} | collective-permute-start | bytes 417800 | tf_op jit(solution)/shard_map/ppermute | solution.py:383
  42.7 0.7 %last_own.1 = (f32[256,1280]{1,0:T(8,128)S(1)}, f32[256,640]{1,0:T(8,128)S(1)}) custom-call(s32[4,4]{1,0:T(4,128)S(1)} %copy-done.5, bf16[256,640]{1,0:T(8,128)(2,1)S(1)} %collective-permute-done.1.ka_ref, bf16[256,384]{1,0:T(8,128)(2,1)S(1)} %collective-permute-done.2.kb_low, bf16[256,256]{1,0:T(8,128)(2,1)S(1)} %collective-permute-done.3.kb_high, ...), custom_call_target="tpu_custom_call" | custom-call | flops 1 | bytes 1 | tf_op jit(solution)/shard_map/last_own/pallas_call | solution.py:146
  43.4 6.6 %collective-permute-done.13.msg_ref = bf16[272,384]{1,0:T(8,128)(2,1)S(1)} collective-permute-done((bf16[272,384]{1,0:T(8,128)(2,1)S(1)}, bf16[272,384]{1,0:T(8,128)(2,1)S(1)}, u32[]{:S(2)}, u32[]{:S(2)}) %collective-permute-start.13) | collective-permute-done | bytes 208928 | tf_op jit(solution)/shard_map/ppermute | solution.py:383
  50.0 1.0 %join0.1.refs_0_ = bf16[256,384]{1,0:T(8,128)(2,1)S(1)} custom-call(s32[4,4]{1,0:T(4,128)S(1)} %copy-done.5, f32[256,1280]{1,0:T(8,128)S(1)} %get-tuple-element.48.acc_ref, f32[256,640]{1,0:T(8,128)S(1)} %get-tuple-element.49.top_ref, bf16[272,384]{1,0:T(8,128)(2,1)S(1)} %collective-permute-done.13.msg_ref), custom_call_target="tpu_custom_call" | custom-call | flops 1 | bytes 1 | tf_op jit(solution)/shard_map/join0/pallas_call | solution.py:146
  51.0 1.6 %collective-permute-start.18 = (bf16[256,384]{1,0:T(8,128)(2,1)S(1)}, bf16[256,384]{1,0:T(8,128)(2,1)S(1)}, u32[]{:S(2)}, u32[]{:S(2)}) collective-permute-start(bf16[256,384]{1,0:T(8,128)(2,1)S(1)} %join0.1.refs_0_), channel_id=1, source_target_pairs={{0,2},{2,0},{1,3},{3,1},{4,6},{6,4},{5,7},{7,5},{8,10},{10,8},{9,1... | collective-permute-start | bytes 589832 | tf_op jit(solution)/shard_map/ppermute | solution.py:392
  52.6 1.1 %join3.1.refs_1_ = bf16[256,256]{1,0:T(8,128)(2,1)S(1)} custom-call(s32[4,4]{1,0:T(4,128)S(1)} %copy-done.5, f32[256,1280]{1,0:T(8,128)S(1)} %get-tuple-element.48.acc_ref, f32[256,640]{1,0:T(8,128)S(1)} %get-tuple-element.49.top_ref, bf16[272,256]{1,0:T(8,128)(2,1)S(1)} %collective-permute-done.12.msg_ref), custom_call_target="tpu_custom_call" | custom-call | flops 1 | bytes 1 | tf_op jit(solution)/shard_map/join3/pallas_call | solution.py:146
  53.7 1.6 %collective-permute-start.14 = (bf16[256,256]{1,0:T(8,128)(2,1)S(1)}, bf16[256,256]{1,0:T(8,128)(2,1)S(1)}, u32[]{:S(2)}, u32[]{:S(2)}) collective-permute-start(bf16[256,256]{1,0:T(8,128)(2,1)S(1)} %join3.1.refs_1_), channel_id=1, source_target_pairs={{0,2},{2,0},{1,3},{3,1},{4,6},{6,4},{5,7},{7,5},{8,10},{10,8},{9,1... | collective-permute-start | bytes 393224 | tf_op jit(solution)/shard_map/ppermute | solution.py:392
  55.3 1.7 %project_most.1.refs_5_ = f32[256,2560]{1,0:T(8,128)S(1)} custom-call(s32[4]{0:T(128)S(1)} %copy-done.7, bf16[256,384]{1,0:T(8,128)(2,1)S(1)} %join0.1.refs_0_, bf16[256,256]{1,0:T(8,128)(2,1)S(1)} %join3.1.refs_1_, bf16[640,2560]{1,0:T(8,128)(2,1)S(1)} %copy-done, bf16[640,2560]{1,0:T(8,128)(2,1)S(1)} %collective-permute-done.15.refs_3_.refs_2_, ...), custom_call_target="tpu_custom_call" | custom-call | flops 1 | bytes 1 | tf_op jit(solution)/shard_map/project_most/pallas_call | solution.py:317
  57.1 1.0 %collective-permute-done.18.refs_0_ = bf16[256,384]{1,0:T(8,128)(2,1)S(1)} collective-permute-done((bf16[256,384]{1,0:T(8,128)(2,1)S(1)}, bf16[256,384]{1,0:T(8,128)(2,1)S(1)}, u32[]{:S(2)}, u32[]{:S(2)}) %collective-permute-start.18) | collective-permute-done | bytes 196640 | tf_op jit(solution)/shard_map/ppermute | solution.py:392
  58.1 1.4 %project_more.1.refs_5_ = f32[256,2560]{1,0:T(8,128)S(1)} custom-call(s32[4]{0:T(128)S(1)} %copy-done.7, bf16[256,384]{1,0:T(8,128)(2,1)S(1)} %collective-permute-done.18.refs_0_, bf16[640,2560]{1,0:T(8,128)(2,1)S(1)} %copy-done, bf16[640,2560]{1,0:T(8,128)(2,1)S(1)} %collective-permute-done.15.refs_3_.refs_2_, ...), custom_call_target="tpu_custom_call" | custom-call | flops 1 | bytes 1 | tf_op jit(solution)/shard_map/project_more/pallas_call | solution.py:317
  59.8 1.9 %project_last.1 = bf16[256,2560]{1,0:T(8,128)(2,1)} custom-call(s32[4]{0:T(128)S(1)} %copy-done.7, bf16[256,256]{1,0:T(8,128)(2,1)S(1)} %collective-permute-done.14.refs_0_, bf16[640,2560]{1,0:T(8,128)(2,1)S(1)} %copy-done, bf16[640,2560]{1,0:T(8,128)(2,1)S(1)} %collective-permute-done.15.refs_3_.refs_2_, ...), custom_call_target="tpu_custom_call" | custom-call | flops 1 | bytes 1 | tf_op jit(solution)/shard_map/project_last/pallas_call | solution.py:317
  (35 shorter events, 3.0 us)
Async XLA Ops:
  0.0 25.1 %collective-permute-start.16 = (bf16[640,2560]{1,0:T(8,128)(2,1)}, bf16[640,2560]{1,0:T(8,128)(2,1)S(1)}, u32[]{:S(2)}, u32[]{:S(2)}) collective-permute-start(bf16[640,2560]{1,0:T(8,128)(2,1)} %refs_1_.3), channel_id=1, source_target_pairs={{1,2},{2,1},{5,6},{6,5},{9,10},{10,9},{13,14},{14,13},{17,18},{18,... | collective-permute-start | bytes 9830408 | tf_op jit(solution)/shard_map/ppermute | solution.py:359
  0.9 7.7 %collective-permute-start = (bf16[256,640]{1,0:T(8,128)(2,1)}, bf16[256,640]{1,0:T(8,128)(2,1)S(1)}, u32[]{:S(2)}, u32[]{:S(2)}) collective-permute-start(bf16[256,640]{1,0:T(8,128)(2,1)} %k_ref.3), channel_id=1, source_target_pairs={{0,4},{4,8},{1,5},{5,9},{2,6},{6,10},{3,7},{7,11},{16,20},{20,24},... | collective-permute-start | bytes 983048 | tf_op jit(solution)/shard_map/ppermute | solution.py:352
  1.6 7.7 %collective-permute-start.8 = (bf16[256,640]{1,0:T(8,128)(2,1)}, bf16[256,640]{1,0:T(8,128)(2,1)S(1)}, u32[]{:S(2)}, u32[]{:S(2)}) collective-permute-start(bf16[256,640]{1,0:T(8,128)(2,1)} %q_ref), channel_id=1, source_target_pairs={{0,1},{1,0},{2,3},{3,2},{4,5},{5,4},{6,7},{7,6},{8,9},{9,8},{10,11... | collective-permute-start | bytes 983048 | tf_op jit(solution)/shard_map/ppermute | solution.py:355
  4.3 10.2 %collective-permute-start.4 = (bf16[256,640]{1,0:T(8,128)(2,1)}, bf16[256,640]{1,0:T(8,128)(2,1)S(1)}, u32[]{:S(2)}, u32[]{:S(2)}) collective-permute-start(bf16[256,640]{1,0:T(8,128)(2,1)} %v_ref.3), channel_id=1, source_target_pairs={{0,4},{4,8},{1,5},{5,9},{2,6},{6,10},{3,7},{7,11},{16,20},{20,24},... | collective-permute-start | bytes 983048 | tf_op jit(solution)/shard_map/ppermute | solution.py:352
  4.9 11.0 %collective-permute-start.7 = (bf16[256,640]{1,0:T(8,128)(2,1)}, bf16[256,640]{1,0:T(8,128)(2,1)S(1)}, u32[]{:S(2)}, u32[]{:S(2)}) collective-permute-start(bf16[256,640]{1,0:T(8,128)(2,1)} %q_ref), channel_id=1, source_target_pairs={{12,8},{13,9},{14,10},{15,11},{28,24},{29,25},{30,26},{31,27}} | collective-permute-start | bytes 983048 | tf_op jit(solution)/shard_map/ppermute | solution.py:360
  8.6 8.1 %collective-permute-start.1 = (bf16[256,640]{1,0:T(8,128)(2,1)S(1)}, bf16[256,640]{1,0:T(8,128)(2,1)S(1)}, u32[]{:S(2)}, u32[]{:S(2)}) collective-permute-start(bf16[256,640]{1,0:T(8,128)(2,1)S(1)} %collective-permute-done.k_ref), channel_id=1, source_target_pairs={{4,8},{5,9},{6,10},{7,11},{20,24},{21,25},{22,26},{23,27}} | collective-permute-start | bytes 983048 | tf_op jit(solution)/shard_map/ppermute | solution.py:352
  9.3 1.0 %copy-start.1 = (bf16[256,640]{1,0:T(8,128)(2,1)S(1)}, bf16[256,640]{1,0:T(8,128)(2,1)}, u32[]{:S(2)}) copy-start(bf16[256,640]{1,0:T(8,128)(2,1)} %q_ref) | copy-start | bytes 983044
  10.2 1.0 %copy-start.3 = (bf16[256,640]{1,0:T(8,128)(2,1)S(1)}, bf16[256,640]{1,0:T(8,128)(2,1)}, u32[]{:S(2)}) copy-start(bf16[256,640]{1,0:T(8,128)(2,1)} %k_ref.3) | copy-start | bytes 983044
  11.2 1.0 %copy-start.4 = (bf16[256,640]{1,0:T(8,128)(2,1)S(1)}, bf16[256,640]{1,0:T(8,128)(2,1)}, u32[]{:S(2)}) copy-start(bf16[256,640]{1,0:T(8,128)(2,1)} %v_ref.3) | copy-start | bytes 983044
  12.2 0.7 %copy-start.5 = (s32[4,4]{1,0:T(4,128)S(1)}, s32[4,4]{1,0:T(4,128)}, u32[]{:S(2)}) copy-start(s32[4,4]{1,0:T(4,128)} %mask_ref.15) | copy-start | bytes 196
  12.9 5.8 %copy-start.2 = (bf16[256,640]{1,0:T(8,128)(2,1)S(1)}, bf16[256,640]{1,0:T(8,128)(2,1)}, u32[]{:S(2)}) copy-start(bf16[256,640]{1,0:T(8,128)(2,1)} %q_ref) | copy-start | bytes 983044
  16.0 1.6 %collective-permute-start.9 = (bf16[256,640]{1,0:T(8,128)(2,1)S(1)}, bf16[256,640]{1,0:T(8,128)(2,1)S(1)}, u32[]{:S(2)}, u32[]{:S(2)}) collective-permute-start(bf16[256,640]{1,0:T(8,128)(2,1)S(1)} %collective-permute-done.7.refs_0_.q_ref), channel_id=1, source_target_pairs={{0,1},{1,0},{2,3},{3,2},{4,5},{5,4},{6,7},{7,6},{8,9},{9,8},{10,11... | collective-permute-start | bytes 983048 | tf_op jit(solution)/shard_map/ppermute | solution.py:355
  16.0 4.3 %collective-permute-start.5 = (bf16[256,640]{1,0:T(8,128)(2,1)S(1)}, bf16[256,640]{1,0:T(8,128)(2,1)S(1)}, u32[]{:S(2)}, u32[]{:S(2)}) collective-permute-start(bf16[256,640]{1,0:T(8,128)(2,1)S(1)} %collective-permute-done.4.v_ref), channel_id=1, source_target_pairs={{4,8},{5,9},{6,10},{7,11},{20,24},{21,25},{22,26},{23,27}} | collective-permute-start | bytes 983048 | tf_op jit(solution)/shard_map/ppermute | solution.py:352
  16.7 2.0 %collective-permute-start.2 = (bf16[256,384]{1,0:T(8,128)(2,1)S(1)}, bf16[256,384]{1,0:T(8,128)(2,1)S(1)}, u32[]{:S(2)}, u32[]{:S(2)}) collective-permute-start(bf16[256,384]{1,0:T(8,128)(2,1)S(1)} %slice.8), channel_id=1, source_target_pairs={{0,1},{1,0},{2,3},{3,2},{4,5},{5,4},{6,7},{7,6},{8,9},{9,8},{10,11... | collective-permute-start | bytes 589832 | tf_op jit(solution)/shard_map/ppermute | solution.py:355
  17.3 1.4 %collective-permute-start.3 = (bf16[256,256]{1,0:T(8,128)(2,1)S(1)}, bf16[256,256]{1,0:T(8,128)(2,1)S(1)}, u32[]{:S(2)}, u32[]{:S(2)}) collective-permute-start(bf16[256,256]{1,0:T(8,128)(2,1)S(1)} %slice.9), channel_id=1, source_target_pairs={{0,1},{1,0},{2,3},{3,2},{4,5},{5,4},{6,7},{7,6},{8,9},{9,8},{10,11... | collective-permute-start | bytes 393224 | tf_op jit(solution)/shard_map/ppermute | solution.py:355
  19.8 1.7 %collective-permute-start.10 = (bf16[272,640]{1,0:T(8,128)(2,1)S(1)}, bf16[272,640]{1,0:T(8,128)(2,1)S(1)}, u32[]{:S(2)}, u32[]{:S(2)}) collective-permute-start(bf16[272,640]{1,0:T(8,128)(2,1)S(1)} %get-tuple-element.37), channel_id=1, source_target_pairs={{0,1},{1,0},{2,3},{3,2},{4,5},{5,4},{6,7},{7,6},{8,9},{9,8},{10,11... | collective-permute-start | bytes 1044488 | tf_op jit(solution)/shard_map/ppermute | solution.py:355
  20.0 2.0 %collective-permute-start.11 = (bf16[272,640]{1,0:T(8,128)(2,1)S(1)}, bf16[272,640]{1,0:T(8,128)(2,1)S(1)}, u32[]{:S(2)}, u32[]{:S(2)}) collective-permute-start(bf16[272,640]{1,0:T(8,128)(2,1)S(1)} %get-tuple-element.40), channel_id=1, source_target_pairs={{0,1},{1,0},{2,3},{3,2},{4,5},{5,4},{6,7},{7,6},{8,9},{9,8},{10,11... | collective-permute-start | bytes 1044488 | tf_op jit(solution)/shard_map/ppermute | solution.py:355
  20.3 2.7 %collective-permute-start.6 = (bf16[256,640]{1,0:T(8,128)(2,1)S(1)}, bf16[256,640]{1,0:T(8,128)(2,1)S(1)}, u32[]{:S(2)}, u32[]{:S(2)}) collective-permute-start(bf16[256,640]{1,0:T(8,128)(2,1)S(1)} %collective-permute-done.5.va_ref), channel_id=1, source_target_pairs={{0,1},{1,0},{2,3},{3,2},{4,5},{5,4},{6,7},{7,6},{8,9},{9,8},{10,11... | collective-permute-start | bytes 983048 | tf_op jit(solution)/shard_map/ppermute | solution.py:355
  23.0 1.9 %copy-start = (bf16[640,2560]{1,0:T(8,128)(2,1)S(1)}, bf16[640,2560]{1,0:T(8,128)(2,1)}, u32[]{:S(2)}) copy-start(bf16[640,2560]{1,0:T(8,128)(2,1)} %refs_1_.3) | copy-start | bytes 9830404
  24.9 30.4 %collective-permute-start.15 = (bf16[640,2560]{1,0:T(8,128)(2,1)S(1)}, bf16[640,2560]{1,0:T(8,128)(2,1)S(1)}, u32[]{:S(2)}, u32[]{:S(2)}) collective-permute-start(bf16[640,2560]{1,0:T(8,128)(2,1)S(1)} %copy-done), channel_id=1, source_target_pairs={{0,1},{1,0},{2,3},{3,2},{4,5},{5,4},{6,7},{7,6},{8,9},{9,8},{10,11... | collective-permute-start | bytes 9830408 | tf_op jit(solution)/shard_map/ppermute | solution.py:355
  25.1 30.2 %collective-permute-start.17 = (bf16[640,2560]{1,0:T(8,128)(2,1)S(1)}, bf16[640,2560]{1,0:T(8,128)(2,1)S(1)}, u32[]{:S(2)}, u32[]{:S(2)}) collective-permute-start(bf16[640,2560]{1,0:T(8,128)(2,1)S(1)} %collective-permute-done.16.refs_4_.refs_3_), channel_id=1, source_target_pairs={{0,1},{1,0},{2,3},{3,2},{4,5},{5,4},{6,7},{7,6},{8,9},{9,8},{10,11... | collective-permute-start | bytes 9830408 | tf_op jit(solution)/shard_map/ppermute | solution.py:355
  40.1 9.9 %collective-permute-start.13 = (bf16[272,384]{1,0:T(8,128)(2,1)S(1)}, bf16[272,384]{1,0:T(8,128)(2,1)S(1)}, u32[]{:S(2)}, u32[]{:S(2)}) collective-permute-start(bf16[272,384]{1,0:T(8,128)(2,1)S(1)} %get-tuple-element.43), channel_id=1, source_target_pairs={{8,12},{9,13},{10,14},{11,15},{24,28},{25,29},{26,30},{27,31}} | collective-permute-start | bytes 626696 | tf_op jit(solution)/shard_map/ppermute | solution.py:383
  41.4 11.2 %collective-permute-start.12 = (bf16[272,256]{1,0:T(8,128)(2,1)S(1)}, bf16[272,256]{1,0:T(8,128)(2,1)S(1)}, u32[]{:S(2)}, u32[]{:S(2)}) collective-permute-start(bf16[272,256]{1,0:T(8,128)(2,1)S(1)} %get-tuple-element.44), channel_id=1, source_target_pairs={{8,12},{9,13},{10,14},{11,15},{24,28},{25,29},{26,30},{27,31}} | collective-permute-start | bytes 417800 | tf_op jit(solution)/shard_map/ppermute | solution.py:383
  43.4 11.9 %copy-start.7 = (s32[4]{0:T(128)S(1)}, s32[4]{0:T(128)}, u32[]{:S(2)}) copy-start(s32[4]{0:T(128)} %step_ref.5) | copy-start | bytes 52
  51.0 7.1 %collective-permute-start.18 = (bf16[256,384]{1,0:T(8,128)(2,1)S(1)}, bf16[256,384]{1,0:T(8,128)(2,1)S(1)}, u32[]{:S(2)}, u32[]{:S(2)}) collective-permute-start(bf16[256,384]{1,0:T(8,128)(2,1)S(1)} %join0.1.refs_0_), channel_id=1, source_target_pairs={{0,2},{2,0},{1,3},{3,1},{4,6},{6,4},{5,7},{7,5},{8,10},{10,8},{9,1... | collective-permute-start | bytes 589832 | tf_op jit(solution)/shard_map/ppermute | solution.py:392
  53.7 6.1 %collective-permute-start.14 = (bf16[256,256]{1,0:T(8,128)(2,1)S(1)}, bf16[256,256]{1,0:T(8,128)(2,1)S(1)}, u32[]{:S(2)}, u32[]{:S(2)}) collective-permute-start(bf16[256,256]{1,0:T(8,128)(2,1)S(1)} %join3.1.refs_1_), channel_id=1, source_target_pairs={{0,2},{2,0},{1,3},{3,1},{4,6},{6,4},{5,7},{7,5},{8,10},{10,8},{9,1... | collective-permute-start | bytes 393224 | tf_op jit(solution)/shard_map/ppermute | solution.py:392
  57.0 2.8 %copy-start.6 = (f32[4,2560]{1,0:T(4,128)S(1)}, f32[4,2560]{1,0:T(4,128)}, u32[]{:S(2)}) copy-start(f32[4,2560]{1,0:T(4,128)} %refs_6_.1) | copy-start | bytes 122884

commit v3 on v2

--- a/solution.py
+++ b/solution.py
@@ -270,7 +270,7 @@
     return call(kernel, "join" + str(part_of_heads[0]), [jax.ShapeDtypeStruct(shape, jnp.bfloat16)], mask, [*state, message])[0]
 
 
-TILE = 512
+TILE = 256
 
 
 def project_kernel(lows, step_ref, *refs):

time: 62.5 us -> 62.5 us (level)
  no operation moved by 1% of the time
where the time goes in v3:
time: 62.5 us; the launch traced here: 61.9 us
  starting transfers between devices  32.2 us (52%)
  Pallas kernels  13 us (21%)
  waiting for transfers between devices  11.4 us (18%)
  local copies, waits for them, and re-layouts  4.95 us (8%)
    ppermute x9, starting transfers between devices, across(): return lax.ppermute(x, 'seq', swap_pairs(cores))  19.2 us
    pallas_call x8, Pallas kernels, call(): pl.pallas_call(kernel, out_shape=out_shape, in_specs=[pl.BlockSpec(memory...  7.96 us
    ppermute x2, waiting for transfers between devices, on_device(): sent = [lax.ppermute(x, 'span', back_up) for x in messages]  6.59 us
    pallas_call x3, Pallas kernels, project(): pl.pallas_call(functools.partial(project_kernel, [(low, own) for _, low,...  5.04 us
    unnamed x16, local copies, waits for them, and re-layouts  4.91 us
    ppermute x1, starting transfers between devices, on_device(): asked = lax.ppermute(query_rows, 'span', [(spans - 1, spans - 2)])  3.59 us
    ppermute x2, starting transfers between devices, on_device(): theirs = [lax.ppermute(x, 'head', swap_pairs(sides)) for x in mine]  3.23 us
    ppermute x4, starting transfers between devices, up(): lax.ppermute(x, 'span', [(i, i + 1) for i in range(step - 1, spans - 2)])  2.7 us
  transfers between devices with their start and end apart: 19, of which 8 were waited for; matrix products, arithmetic and copies ran while one was open for 0% of the time, Pallas kernels for 18%

profile of v3, /device:TPU:28, one launch (start us, length us, event | category | flops | bytes accessed | tf_op | source)
XLA Modules:
  0.0 61.9 jit_solution(4875956186354993413)
XLA Ops:
  0.0 0.9 %collective-permute-start.16 = (bf16[640,2560]{1,0:T(8,128)(2,1)}, bf16[640,2560]{1,0:T(8,128)(2,1)S(1)}, u32[]{:S(2)}, u32[]{:S(2)}) collective-permute-start(bf16[640,2560]{1,0:T(8,128)(2,1)} %refs_1_.3), channel_id=1, source_target_pairs={{1,2},{2,1},{5,6},{6,5},{9,10},{10,9},{13,14},{14,13},{17,18},{18,... | collective-permute-start | bytes 9830408 | tf_op jit(solution)/shard_map/ppermute | solution.py:359
  0.9 0.7 %collective-permute-start = (bf16[256,640]{1,0:T(8,128)(2,1)}, bf16[256,640]{1,0:T(8,128)(2,1)S(1)}, u32[]{:S(2)}, u32[]{:S(2)}) collective-permute-start(bf16[256,640]{1,0:T(8,128)(2,1)} %k_ref.3), channel_id=1, source_target_pairs={{0,4},{4,8},{1,5},{5,9},{2,6},{6,10},{3,7},{7,11},{16,20},{20,24},... | collective-permute-start | bytes 983048 | tf_op jit(solution)/shard_map/ppermute | solution.py:352
  1.6 2.7 %collective-permute-start.8 = (bf16[256,640]{1,0:T(8,128)(2,1)}, bf16[256,640]{1,0:T(8,128)(2,1)S(1)}, u32[]{:S(2)}, u32[]{:S(2)}) collective-permute-start(bf16[256,640]{1,0:T(8,128)(2,1)} %q_ref), channel_id=1, source_target_pairs={{0,1},{1,0},{2,3},{3,2},{4,5},{5,4},{6,7},{7,6},{8,9},{9,8},{10,11... | collective-permute-start | bytes 983048 | tf_op jit(solution)/shard_map/ppermute | solution.py:355
  4.3 0.7 %collective-permute-start.4 = (bf16[256,640]{1,0:T(8,128)(2,1)}, bf16[256,640]{1,0:T(8,128)(2,1)S(1)}, u32[]{:S(2)}, u32[]{:S(2)}) collective-permute-start(bf16[256,640]{1,0:T(8,128)(2,1)} %v_ref.3), channel_id=1, source_target_pairs={{0,4},{4,8},{1,5},{5,9},{2,6},{6,10},{3,7},{7,11},{16,20},{20,24},... | collective-permute-start | bytes 983048 | tf_op jit(solution)/shard_map/ppermute | solution.py:352
  4.9 3.6 %collective-permute-start.7 = (bf16[256,640]{1,0:T(8,128)(2,1)}, bf16[256,640]{1,0:T(8,128)(2,1)S(1)}, u32[]{:S(2)}, u32[]{:S(2)}) collective-permute-start(bf16[256,640]{1,0:T(8,128)(2,1)} %q_ref), channel_id=1, source_target_pairs={{12,8},{13,9},{14,10},{15,11},{28,24},{29,25},{30,26},{31,27}} | collective-permute-start | bytes 983048 | tf_op jit(solution)/shard_map/ppermute | solution.py:360
  8.6 0.7 %collective-permute-start.1 = (bf16[256,640]{1,0:T(8,128)(2,1)S(1)}, bf16[256,640]{1,0:T(8,128)(2,1)S(1)}, u32[]{:S(2)}, u32[]{:S(2)}) collective-permute-start(bf16[256,640]{1,0:T(8,128)(2,1)S(1)} %collective-permute-done.k_ref), channel_id=1, source_target_pairs={{4,8},{5,9},{6,10},{7,11},{20,24},{21,25},{22,26},{23,27}} | collective-permute-start | bytes 983048 | tf_op jit(solution)/shard_map/ppermute | solution.py:352
  9.3 1.0 %copy-done.1 = bf16[256,640]{1,0:T(8,128)(2,1)S(1)} copy-done((bf16[256,640]{1,0:T(8,128)(2,1)S(1)}, bf16[256,640]{1,0:T(8,128)(2,1)}, u32[]{:S(2)}) %copy-start.1) | copy-done | bytes 327704
  10.2 1.0 %copy-done.3 = bf16[256,640]{1,0:T(8,128)(2,1)S(1)} copy-done((bf16[256,640]{1,0:T(8,128)(2,1)S(1)}, bf16[256,640]{1,0:T(8,128)(2,1)}, u32[]{:S(2)}) %copy-start.3) | copy-done | bytes 327704
  11.2 1.0 %copy-done.4 = bf16[256,640]{1,0:T(8,128)(2,1)S(1)} copy-done((bf16[256,640]{1,0:T(8,128)(2,1)S(1)}, bf16[256,640]{1,0:T(8,128)(2,1)}, u32[]{:S(2)}) %copy-start.4) | copy-done | bytes 327704
  12.2 0.7 %copy-done.5 = s32[4,4]{1,0:T(4,128)S(1)} copy-done((s32[4,4]{1,0:T(4,128)S(1)}, s32[4,4]{1,0:T(4,128)}, u32[]{:S(2)}) %copy-start.5) | copy-done | bytes 88
  12.9 1.6 %attend_own0.1 = (f32[512,1280]{1,0:T(8,128)S(1)}, f32[512,640]{1,0:T(8,128)S(1)}) custom-call(s32[4,4]{1,0:T(4,128)S(1)} %copy-done.5, bf16[256,640]{1,0:T(8,128)(2,1)S(1)} %copy-done.3, bf16[256,640]{1,0:T(8,128)(2,1)S(1)} %copy-done.4, bf16[256,640]{1,0:T(8,128)(2,1)S(1)} %copy-done.1, bf16[256,640]{1,0:T(8,128)(2,1)S(1)} %collective-permute-done.8.refs_1_.refs_3_), custom_call_target="tpu_custom_call" | custom-call | flops 1 | bytes 1 | tf_op jit(solution)/shard_map/attend_own0/pallas_call | solution.py:146
  14.5 1.5 %collective-permute-done.7.refs_0_.q_ref = bf16[256,640]{1,0:T(8,128)(2,1)S(1)} collective-permute-done((bf16[256,640]{1,0:T(8,128)(2,1)}, bf16[256,640]{1,0:T(8,128)(2,1)S(1)}, u32[]{:S(2)}, u32[]{:S(2)}) %collective-permute-start.7) | collective-permute-done | bytes 327712 | tf_op jit(solution)/shard_map/ppermute | solution.py:360
  16.0 0.7 %collective-permute-start.5 = (bf16[256,640]{1,0:T(8,128)(2,1)S(1)}, bf16[256,640]{1,0:T(8,128)(2,1)S(1)}, u32[]{:S(2)}, u32[]{:S(2)}) collective-permute-start(bf16[256,640]{1,0:T(8,128)(2,1)S(1)} %collective-permute-done.4.v_ref), channel_id=1, source_target_pairs={{4,8},{5,9},{6,10},{7,11},{20,24},{21,25},{22,26},{23,27}} | collective-permute-start | bytes 983048 | tf_op jit(solution)/shard_map/ppermute | solution.py:352
  17.6 0.8 %attend_lent0.1 = (f32[512,1280]{1,0:T(8,128)S(1)}, f32[512,640]{1,0:T(8,128)S(1)}) custom-call(s32[4,4]{1,0:T(4,128)S(1)} %copy-done.5, bf16[256,640]{1,0:T(8,128)(2,1)S(1)} %copy-done.3, bf16[256,640]{1,0:T(8,128)(2,1)S(1)} %copy-done.4, bf16[256,640]{1,0:T(8,128)(2,1)S(1)} %collective-permute-done.7.refs_0_.q_ref, ...), custom_call_target="tpu_custom_call" | custom-call | flops 1 | bytes 1 | tf_op jit(solution)/shard_map/attend_lent0/pallas_call | solution.py:146
  18.7 1.1 %attend_lent_own1.1 = (f32[512,1280]{1,0:T(8,128)S(1)}, f32[512,640]{1,0:T(8,128)S(1)}, f32[512,1280]{1,0:T(8,128)S(1)}, f32[512,640]{1,0:T(8,128)S(1)}, bf16[27...) custom-call(s32[4,4]{1,0:T(4,128)S(1)} %copy-done.5, ...), custom_call_target="tpu_custom_call", output_to_operand_aliasing={{0}: (7, {}), {1}: (8, {}), {2}: (9, {}), {3}: (10, {})} | custom-call | flops 1 | bytes 1 | tf_op jit(solution)/shard_map/attend_lent_own1/pallas_call | solution.py:146
  20.5 0.9 %collective-permute-done.10.refs_2_ = bf16[272,640]{1,0:T(8,128)(2,1)S(1)} collective-permute-done((bf16[272,640]{1,0:T(8,128)(2,1)S(1)}, bf16[272,640]{1,0:T(8,128)(2,1)S(1)}, u32[]{:S(2)}, u32[]{:S(2)}) %collective-permute-start.10) | collective-permute-done | bytes 348192 | tf_op jit(solution)/shard_map/ppermute | solution.py:355
  21.9 1.1 %fold.1 = (f32[256,1280]{1,0:T(8,128)S(1)}, f32[256,640]{1,0:T(8,128)S(1)}, f32[256,1280]{1,0:T(8,128)S(1)}, f32[256,640]{1,0:T(8,128)S(1)}) custom-call(s32[4,4]{1,0:T(4,128)S(1)} %copy-done.5, f32[512,1280]{1,0:T(8,128)S(1)} %get-tuple-element.35.refs_0_, f32[512,640]{1,0:T(8,128)S(1)} %get-tuple-element.36.refs_1_, ...), custom_call_target="tpu_custom_call" | custom-call | flops 1 | bytes 1 | tf_op jit(solution)/shard_map/fold/pallas_call | solution.py:146
  23.0 0.6 last_lent.1
  23.6 1.3 %copy-done = bf16[640,2560]{1,0:T(8,128)(2,1)S(1)} copy-done((bf16[640,2560]{1,0:T(8,128)(2,1)S(1)}, bf16[640,2560]{1,0:T(8,128)(2,1)}, u32[]{:S(2)}) %copy-start) | copy-done | bytes 3276824
  25.1 14.9 %collective-permute-start.17 = (bf16[640,2560]{1,0:T(8,128)(2,1)S(1)}, bf16[640,2560]{1,0:T(8,128)(2,1)S(1)}, u32[]{:S(2)}, u32[]{:S(2)}) collective-permute-start(bf16[640,2560]{1,0:T(8,128)(2,1)S(1)} %collective-permute-done.16.refs_4_.refs_3_), channel_id=1, source_target_pairs={{0,1},{1,0},{2,3},{3,2},{4,5},{5,4},{6,7},{7,6},{8,9},{9,8},{10,11... | collective-permute-start | bytes 9830408 | tf_op jit(solution)/shard_map/ppermute | solution.py:355
  40.1 1.3 %collective-permute-start.13 = (bf16[272,384]{1,0:T(8,128)(2,1)S(1)}, bf16[272,384]{1,0:T(8,128)(2,1)S(1)}, u32[]{:S(2)}, u32[]{:S(2)}) collective-permute-start(bf16[272,384]{1,0:T(8,128)(2,1)S(1)} %get-tuple-element.43), channel_id=1, source_target_pairs={{8,12},{9,13},{10,14},{11,15},{24,28},{25,29},{26,30},{27,31}} | collective-permute-start | bytes 626696 | tf_op jit(solution)/shard_map/ppermute | solution.py:383
  41.4 1.3 %collective-permute-start.12 = (bf16[272,256]{1,0:T(8,128)(2,1)S(1)}, bf16[272,256]{1,0:T(8,128)(2,1)S(1)}, u32[]{:S(2)}, u32[]{:S(2)}) collective-permute-start(bf16[272,256]{1,0:T(8,128)(2,1)S(1)} %get-tuple-element.44), channel_id=1, source_target_pairs={{8,12},{9,13},{10,14},{11,15},{24,28},{25,29},{26,30},{27,31}} | collective-permute-start | bytes 417800 | tf_op jit(solution)/shard_map/ppermute | solution.py:383
  42.7 0.7 %last_own.1 = (f32[256,1280]{1,0:T(8,128)S(1)}, f32[256,640]{1,0:T(8,128)S(1)}) custom-call(s32[4,4]{1,0:T(4,128)S(1)} %copy-done.5, bf16[256,640]{1,0:T(8,128)(2,1)S(1)} %collective-permute-done.1.ka_ref, bf16[256,384]{1,0:T(8,128)(2,1)S(1)} %collective-permute-done.2.kb_low, bf16[256,256]{1,0:T(8,128)(2,1)S(1)} %collective-permute-done.3.kb_high, ...), custom_call_target="tpu_custom_call" | custom-call | flops 1 | bytes 1 | tf_op jit(solution)/shard_map/last_own/pallas_call | solution.py:146
  43.4 6.6 %collective-permute-done.13.msg_ref = bf16[272,384]{1,0:T(8,128)(2,1)S(1)} collective-permute-done((bf16[272,384]{1,0:T(8,128)(2,1)S(1)}, bf16[272,384]{1,0:T(8,128)(2,1)S(1)}, u32[]{:S(2)}, u32[]{:S(2)}) %collective-permute-start.13) | collective-permute-done | bytes 208928 | tf_op jit(solution)/shard_map/ppermute | solution.py:383
  50.0 1.0 %join0.1.refs_0_ = bf16[256,384]{1,0:T(8,128)(2,1)S(1)} custom-call(s32[4,4]{1,0:T(4,128)S(1)} %copy-done.5, f32[256,1280]{1,0:T(8,128)S(1)} %get-tuple-element.48.acc_ref, f32[256,640]{1,0:T(8,128)S(1)} %get-tuple-element.49.top_ref, bf16[272,384]{1,0:T(8,128)(2,1)S(1)} %collective-permute-done.13.msg_ref), custom_call_target="tpu_custom_call" | custom-call | flops 1 | bytes 1 | tf_op jit(solution)/shard_map/join0/pallas_call | solution.py:146
  51.0 1.6 %collective-permute-start.18 = (bf16[256,384]{1,0:T(8,128)(2,1)S(1)}, bf16[256,384]{1,0:T(8,128)(2,1)S(1)}, u32[]{:S(2)}, u32[]{:S(2)}) collective-permute-start(bf16[256,384]{1,0:T(8,128)(2,1)S(1)} %join0.1.refs_0_), channel_id=1, source_target_pairs={{0,2},{2,0},{1,3},{3,1},{4,6},{6,4},{5,7},{7,5},{8,10},{10,8},{9,1... | collective-permute-start | bytes 589832 | tf_op jit(solution)/shard_map/ppermute | solution.py:392
  52.6 1.1 %join3.1.refs_1_ = bf16[256,256]{1,0:T(8,128)(2,1)S(1)} custom-call(s32[4,4]{1,0:T(4,128)S(1)} %copy-done.5, f32[256,1280]{1,0:T(8,128)S(1)} %get-tuple-element.48.acc_ref, f32[256,640]{1,0:T(8,128)S(1)} %get-tuple-element.49.top_ref, bf16[272,256]{1,0:T(8,128)(2,1)S(1)} %collective-permute-done.12.msg_ref), custom_call_target="tpu_custom_call" | custom-call | flops 1 | bytes 1 | tf_op jit(solution)/shard_map/join3/pallas_call | solution.py:146
  53.7 1.6 %collective-permute-start.14 = (bf16[256,256]{1,0:T(8,128)(2,1)S(1)}, bf16[256,256]{1,0:T(8,128)(2,1)S(1)}, u32[]{:S(2)}, u32[]{:S(2)}) collective-permute-start(bf16[256,256]{1,0:T(8,128)(2,1)S(1)} %join3.1.refs_1_), channel_id=1, source_target_pairs={{0,2},{2,0},{1,3},{3,1},{4,6},{6,4},{5,7},{7,5},{8,10},{10,8},{9,1... | collective-permute-start | bytes 393224 | tf_op jit(solution)/shard_map/ppermute | solution.py:392
  55.3 1.7 %project_most.1.refs_5_ = f32[256,2560]{1,0:T(8,128)S(1)} custom-call(s32[4]{0:T(128)S(1)} %copy-done.7, bf16[256,384]{1,0:T(8,128)(2,1)S(1)} %join0.1.refs_0_, bf16[256,256]{1,0:T(8,128)(2,1)S(1)} %join3.1.refs_1_, bf16[640,2560]{1,0:T(8,128)(2,1)S(1)} %copy-done, bf16[640,2560]{1,0:T(8,128)(2,1)S(1)} %collective-permute-done.15.refs_3_.refs_2_, ...), custom_call_target="tpu_custom_call" | custom-call | flops 1 | bytes 1 | tf_op jit(solution)/shard_map/project_most/pallas_call | solution.py:317
  57.1 1.0 %collective-permute-done.18.refs_0_ = bf16[256,384]{1,0:T(8,128)(2,1)S(1)} collective-permute-done((bf16[256,384]{1,0:T(8,128)(2,1)S(1)}, bf16[256,384]{1,0:T(8,128)(2,1)S(1)}, u32[]{:S(2)}, u32[]{:S(2)}) %collective-permute-start.18) | collective-permute-done | bytes 196640 | tf_op jit(solution)/shard_map/ppermute | solution.py:392
  58.1 1.4 %project_more.1.refs_5_ = f32[256,2560]{1,0:T(8,128)S(1)} custom-call(s32[4]{0:T(128)S(1)} %copy-done.7, bf16[256,384]{1,0:T(8,128)(2,1)S(1)} %collective-permute-done.18.refs_0_, bf16[640,2560]{1,0:T(8,128)(2,1)S(1)} %copy-done, bf16[640,2560]{1,0:T(8,128)(2,1)S(1)} %collective-permute-done.15.refs_3_.refs_2_, ...), custom_call_target="tpu_custom_call" | custom-call | flops 1 | bytes 1 | tf_op jit(solution)/shard_map/project_more/pallas_call | solution.py:317
  59.8 1.9 %project_last.1 = bf16[256,2560]{1,0:T(8,128)(2,1)} custom-call(s32[4]{0:T(128)S(1)} %copy-done.7, bf16[256,256]{1,0:T(8,128)(2,1)S(1)} %collective-permute-done.14.refs_0_, bf16[640,2560]{1,0:T(8,128)(2,1)S(1)} %copy-done, bf16[640,2560]{1,0:T(8,128)(2,1)S(1)} %collective-permute-done.15.refs_3_.refs_2_, ...), custom_call_target="tpu_custom_call" | custom-call | flops 1 | bytes 1 | tf_op jit(solution)/shard_map/project_last/pallas_call | solution.py:317
  (35 shorter events, 3.0 us)
Async XLA Ops:
  0.0 25.1 %collective-permute-start.16 = (bf16[640,2560]{1,0:T(8,128)(2,1)}, bf16[640,2560]{1,0:T(8,128)(2,1)S(1)}, u32[]{:S(2)}, u32[]{:S(2)}) collective-permute-start(bf16[640,2560]{1,0:T(8,128)(2,1)} %refs_1_.3), channel_id=1, source_target_pairs={{1,2},{2,1},{5,6},{6,5},{9,10},{10,9},{13,14},{14,13},{17,18},{18,... | collective-permute-start | bytes 9830408 | tf_op jit(solution)/shard_map/ppermute | solution.py:359
  0.9 7.7 %collective-permute-start = (bf16[256,640]{1,0:T(8,128)(2,1)}, bf16[256,640]{1,0:T(8,128)(2,1)S(1)}, u32[]{:S(2)}, u32[]{:S(2)}) collective-permute-start(bf16[256,640]{1,0:T(8,128)(2,1)} %k_ref.3), channel_id=1, source_target_pairs={{0,4},{4,8},{1,5},{5,9},{2,6},{6,10},{3,7},{7,11},{16,20},{20,24},... | collective-permute-start | bytes 983048 | tf_op jit(solution)/shard_map/ppermute | solution.py:352
  1.6 7.7 %collective-permute-start.8 = (bf16[256,640]{1,0:T(8,128)(2,1)}, bf16[256,640]{1,0:T(8,128)(2,1)S(1)}, u32[]{:S(2)}, u32[]{:S(2)}) collective-permute-start(bf16[256,640]{1,0:T(8,128)(2,1)} %q_ref), channel_id=1, source_target_pairs={{0,1},{1,0},{2,3},{3,2},{4,5},{5,4},{6,7},{7,6},{8,9},{9,8},{10,11... | collective-permute-start | bytes 983048 | tf_op jit(solution)/shard_map/ppermute | solution.py:355
  4.3 10.2 %collective-permute-start.4 = (bf16[256,640]{1,0:T(8,128)(2,1)}, bf16[256,640]{1,0:T(8,128)(2,1)S(1)}, u32[]{:S(2)}, u32[]{:S(2)}) collective-permute-start(bf16[256,640]{1,0:T(8,128)(2,1)} %v_ref.3), channel_id=1, source_target_pairs={{0,4},{4,8},{1,5},{5,9},{2,6},{6,10},{3,7},{7,11},{16,20},{20,24},... | collective-permute-start | bytes 983048 | tf_op jit(solution)/shard_map/ppermute | solution.py:352
  4.9 11.0 %collective-permute-start.7 = (bf16[256,640]{1,0:T(8,128)(2,1)}, bf16[256,640]{1,0:T(8,128)(2,1)S(1)}, u32[]{:S(2)}, u32[]{:S(2)}) collective-permute-start(bf16[256,640]{1,0:T(8,128)(2,1)} %q_ref), channel_id=1, source_target_pairs={{12,8},{13,9},{14,10},{15,11},{28,24},{29,25},{30,26},{31,27}} | collective-permute-start | bytes 983048 | tf_op jit(solution)/shard_map/ppermute | solution.py:360
  8.6 8.1 %collective-permute-start.1 = (bf16[256,640]{1,0:T(8,128)(2,1)S(1)}, bf16[256,640]{1,0:T(8,128)(2,1)S(1)}, u32[]{:S(2)}, u32[]{:S(2)}) collective-permute-start(bf16[256,640]{1,0:T(8,128)(2,1)S(1)} %collective-permute-done.k_ref), channel_id=1, source_target_pairs={{4,8},{5,9},{6,10},{7,11},{20,24},{21,25},{22,26},{23,27}} | collective-permute-start | bytes 983048 | tf_op jit(solution)/shard_map/ppermute | solution.py:352
  9.3 1.0 %copy-start.1 = (bf16[256,640]{1,0:T(8,128)(2,1)S(1)}, bf16[256,640]{1,0:T(8,128)(2,1)}, u32[]{:S(2)}) copy-start(bf16[256,640]{1,0:T(8,128)(2,1)} %q_ref) | copy-start | bytes 983044
  10.2 1.0 %copy-start.3 = (bf16[256,640]{1,0:T(8,128)(2,1)S(1)}, bf16[256,640]{1,0:T(8,128)(2,1)}, u32[]{:S(2)}) copy-start(bf16[256,640]{1,0:T(8,128)(2,1)} %k_ref.3) | copy-start | bytes 983044
  11.2 1.0 %copy-start.4 = (bf16[256,640]{1,0:T(8,128)(2,1)S(1)}, bf16[256,640]{1,0:T(8,128)(2,1)}, u32[]{:S(2)}) copy-start(bf16[256,640]{1,0:T(8,128)(2,1)} %v_ref.3) | copy-start | bytes 983044
  12.2 0.7 %copy-start.5 = (s32[4,4]{1,0:T(4,128)S(1)}, s32[4,4]{1,0:T(4,128)}, u32[]{:S(2)}) copy-start(s32[4,4]{1,0:T(4,128)} %mask_ref.15) | copy-start | bytes 196
  12.9 5.8 %copy-start.2 = (bf16[256,640]{1,0:T(8,128)(2,1)S(1)}, bf16[256,640]{1,0:T(8,128)(2,1)}, u32[]{:S(2)}) copy-start(bf16[256,640]{1,0:T(8,128)(2,1)} %q_ref) | copy-start | bytes 983044
  16.0 1.6 %collective-permute-start.9 = (bf16[256,640]{1,0:T(8,128)(2,1)S(1)}, bf16[256,640]{1,0:T(8,128)(2,1)S(1)}, u32[]{:S(2)}, u32[]{:S(2)}) collective-permute-start(bf16[256,640]{1,0:T(8,128)(2,1)S(1)} %collective-permute-done.7.refs_0_.q_ref), channel_id=1, source_target_pairs={{0,1},{1,0},{2,3},{3,2},{4,5},{5,4},{6,7},{7,6},{8,9},{9,8},{10,11... | collective-permute-start | bytes 983048 | tf_op jit(solution)/shard_map/ppermute | solution.py:355
  16.0 4.3 %collective-permute-start.5 = (bf16[256,640]{1,0:T(8,128)(2,1)S(1)}, bf16[256,640]{1,0:T(8,128)(2,1)S(1)}, u32[]{:S(2)}, u32[]{:S(2)}) collective-permute-start(bf16[256,640]{1,0:T(8,128)(2,1)S(1)} %collective-permute-done.4.v_ref), channel_id=1, source_target_pairs={{4,8},{5,9},{6,10},{7,11},{20,24},{21,25},{22,26},{23,27}} | collective-permute-start | bytes 983048 | tf_op jit(solution)/shard_map/ppermute | solution.py:352
  16.7 2.0 %collective-permute-start.2 = (bf16[256,384]{1,0:T(8,128)(2,1)S(1)}, bf16[256,384]{1,0:T(8,128)(2,1)S(1)}, u32[]{:S(2)}, u32[]{:S(2)}) collective-permute-start(bf16[256,384]{1,0:T(8,128)(2,1)S(1)} %slice.8), channel_id=1, source_target_pairs={{0,1},{1,0},{2,3},{3,2},{4,5},{5,4},{6,7},{7,6},{8,9},{9,8},{10,11... | collective-permute-start | bytes 589832 | tf_op jit(solution)/shard_map/ppermute | solution.py:355
  17.3 1.4 %collective-permute-start.3 = (bf16[256,256]{1,0:T(8,128)(2,1)S(1)}, bf16[256,256]{1,0:T(8,128)(2,1)S(1)}, u32[]{:S(2)}, u32[]{:S(2)}) collective-permute-start(bf16[256,256]{1,0:T(8,128)(2,1)S(1)} %slice.9), channel_id=1, source_target_pairs={{0,1},{1,0},{2,3},{3,2},{4,5},{5,4},{6,7},{7,6},{8,9},{9,8},{10,11... | collective-permute-start | bytes 393224 | tf_op jit(solution)/shard_map/ppermute | solution.py:355
  19.8 1.7 %collective-permute-start.10 = (bf16[272,640]{1,0:T(8,128)(2,1)S(1)}, bf16[272,640]{1,0:T(8,128)(2,1)S(1)}, u32[]{:S(2)}, u32[]{:S(2)}) collective-permute-start(bf16[272,640]{1,0:T(8,128)(2,1)S(1)} %get-tuple-element.37), channel_id=1, source_target_pairs={{0,1},{1,0},{2,3},{3,2},{4,5},{5,4},{6,7},{7,6},{8,9},{9,8},{10,11... | collective-permute-start | bytes 1044488 | tf_op jit(solution)/shard_map/ppermute | solution.py:355
  20.0 2.0 %collective-permute-start.11 = (bf16[272,640]{1,0:T(8,128)(2,1)S(1)}, bf16[272,640]{1,0:T(8,128)(2,1)S(1)}, u32[]{:S(2)}, u32[]{:S(2)}) collective-permute-start(bf16[272,640]{1,0:T(8,128)(2,1)S(1)} %get-tuple-element.40), channel_id=1, source_target_pairs={{0,1},{1,0},{2,3},{3,2},{4,5},{5,4},{6,7},{7,6},{8,9},{9,8},{10,11... | collective-permute-start | bytes 1044488 | tf_op jit(solution)/shard_map/ppermute | solution.py:355
  20.3 2.7 %collective-permute-start.6 = (bf16[256,640]{1,0:T(8,128)(2,1)S(1)}, bf16[256,640]{1,0:T(8,128)(2,1)S(1)}, u32[]{:S(2)}, u32[]{:S(2)}) collective-permute-start(bf16[256,640]{1,0:T(8,128)(2,1)S(1)} %collective-permute-done.5.va_ref), channel_id=1, source_target_pairs={{0,1},{1,0},{2,3},{3,2},{4,5},{5,4},{6,7},{7,6},{8,9},{9,8},{10,11... | collective-permute-start | bytes 983048 | tf_op jit(solution)/shard_map/ppermute | solution.py:355
  23.0 1.9 %copy-start = (bf16[640,2560]{1,0:T(8,128)(2,1)S(1)}, bf16[640,2560]{1,0:T(8,128)(2,1)}, u32[]{:S(2)}) copy-start(bf16[640,2560]{1,0:T(8,128)(2,1)} %refs_1_.3) | copy-start | bytes 9830404
  24.9 30.4 %collective-permute-start.15 = (bf16[640,2560]{1,0:T(8,128)(2,1)S(1)}, bf16[640,2560]{1,0:T(8,128)(2,1)S(1)}, u32[]{:S(2)}, u32[]{:S(2)}) collective-permute-start(bf16[640,2560]{1,0:T(8,128)(2,1)S(1)} %copy-done), channel_id=1, source_target_pairs={{0,1},{1,0},{2,3},{3,2},{4,5},{5,4},{6,7},{7,6},{8,9},{9,8},{10,11... | collective-permute-start | bytes 9830408 | tf_op jit(solution)/shard_map/ppermute | solution.py:355
  25.1 30.2 %collective-permute-start.17 = (bf16[640,2560]{1,0:T(8,128)(2,1)S(1)}, bf16[640,2560]{1,0:T(8,128)(2,1)S(1)}, u32[]{:S(2)}, u32[]{:S(2)}) collective-permute-start(bf16[640,2560]{1,0:T(8,128)(2,1)S(1)} %collective-permute-done.16.refs_4_.refs_3_), channel_id=1, source_target_pairs={{0,1},{1,0},{2,3},{3,2},{4,5},{5,4},{6,7},{7,6},{8,9},{9,8},{10,11... | collective-permute-start | bytes 9830408 | tf_op jit(solution)/shard_map/ppermute | solution.py:355
  40.1 9.9 %collective-permute-start.13 = (bf16[272,384]{1,0:T(8,128)(2,1)S(1)}, bf16[272,384]{1,0:T(8,128)(2,1)S(1)}, u32[]{:S(2)}, u32[]{:S(2)}) collective-permute-start(bf16[272,384]{1,0:T(8,128)(2,1)S(1)} %get-tuple-element.43), channel_id=1, source_target_pairs={{8,12},{9,13},{10,14},{11,15},{24,28},{25,29},{26,30},{27,31}} | collective-permute-start | bytes 626696 | tf_op jit(solution)/shard_map/ppermute | solution.py:383
  41.4 11.2 %collective-permute-start.12 = (bf16[272,256]{1,0:T(8,128)(2,1)S(1)}, bf16[272,256]{1,0:T(8,128)(2,1)S(1)}, u32[]{:S(2)}, u32[]{:S(2)}) collective-permute-start(bf16[272,256]{1,0:T(8,128)(2,1)S(1)} %get-tuple-element.44), channel_id=1, source_target_pairs={{8,12},{9,13},{10,14},{11,15},{24,28},{25,29},{26,30},{27,31}} | collective-permute-start | bytes 417800 | tf_op jit(solution)/shard_map/ppermute | solution.py:383
  43.4 11.9 %copy-start.7 = (s32[4]{0:T(128)S(1)}, s32[4]{0:T(128)}, u32[]{:S(2)}) copy-start(s32[4]{0:T(128)} %step_ref.5) | copy-start | bytes 52
  51.0 7.1 %collective-permute-start.18 = (bf16[256,384]{1,0:T(8,128)(2,1)S(1)}, bf16[256,384]{1,0:T(8,128)(2,1)S(1)}, u32[]{:S(2)}, u32[]{:S(2)}) collective-permute-start(bf16[256,384]{1,0:T(8,128)(2,1)S(1)} %join0.1.refs_0_), channel_id=1, source_target_pairs={{0,2},{2,0},{1,3},{3,1},{4,6},{6,4},{5,7},{7,5},{8,10},{10,8},{9,1... | collective-permute-start | bytes 589832 | tf_op jit(solution)/shard_map/ppermute | solution.py:392
  53.7 6.1 %collective-permute-start.14 = (bf16[256,256]{1,0:T(8,128)(2,1)S(1)}, bf16[256,256]{1,0:T(8,128)(2,1)S(1)}, u32[]{:S(2)}, u32[]{:S(2)}) collective-permute-start(bf16[256,256]{1,0:T(8,128)(2,1)S(1)} %join3.1.refs_1_), channel_id=1, source_target_pairs={{0,2},{2,0},{1,3},{3,1},{4,6},{6,4},{5,7},{7,5},{8,10},{10,8},{9,1... | collective-permute-start | bytes 393224 | tf_op jit(solution)/shard_map/ppermute | solution.py:392
  57.0 2.8 %copy-start.6 = (f32[4,2560]{1,0:T(4,128)S(1)}, f32[4,2560]{1,0:T(4,128)}, u32[]{:S(2)}) copy-start(f32[4,2560]{1,0:T(4,128)} %refs_6_.1) | copy-start | bytes 122884
